TPU v7x, 32 devices: a whole 2x2x4 slice. The times are simulated.
32 devices in a mesh: gx: 4 (over z), gy: 4 (over x, core), gz: 2 (over y).
Axes of the slice: x: 2, y: 2, z: 4, core: 2. Of those that a mesh axis runs over, the one named last changes fastest.
Arguments:
- features: float32 [4, 8, 2, 128, 256], P('gx', 'gy', 'gz'), may hold values from -82 to 82
- occupancy: int32 [4, 8, 2], P('gx', 'gy', 'gz'), may hold values from 1 to 128, as said below
- dest_bin: int32 [4, 8, 2], P('gx', 'gy', 'gz'), may hold values from 0 to 63, as said below
- query_weight: bfloat16 [256, 256], replicated, may hold values from -0.375 to 0.375
- key_weight: bfloat16 [256, 256], replicated, may hold values from -0.375 to 0.375
- value_weight: bfloat16 [256, 256], replicated, may hold values from -0.375 to 0.375
- out_weight: bfloat16 [256, 256], replicated, may hold values from -0.375 to 0.375
- up_weight: bfloat16 [256, 1024], replicated, may hold values from -0.375 to 0.375
- down_weight: bfloat16 [1024, 256], replicated, may hold values from -0.1875 to 0.1875
- attention_gain: float32 [256], replicated, may hold values from 0.25 to 1.75
- feed_gain: float32 [256], replicated, may hold values from 0.25 to 1.75
Outputs:
- particles: float32 [4, 8, 2, 128, 256], P('gx', 'gy', 'gz')
Inputs may be any that keep to these rules, and one draw needn't show every extreme that they name: `occupancy`: some bin holds 128 live particles. `dest_bin`: A permutation of the bins; every block stays on a device with the same gx and gy index, and each device sends at most 1 block to any one device, a bound that some pair of devices reaches.
All inputs are finite; a program needn't handle non-finite values.
Results may differ from a plain program's by a relative error of at most 0.0065.
The roundings to bfloat16 on the way count: a program that leaves them out, or rounds other values in their place, can miss the bound.
Values may be sent and summed in bfloat16 or wider, within the bound.
No kernel may reach another device: no remote copies, remote signals or barrier semaphores. Data moves between devices by JAX's collectives and lax.ppermute only.
A program may use at most 64 MiB of HBM per device.

v0:
```python
import jax
import jax.numpy as jnp
from jax import lax
from jax.sharding import PartitionSpec as P

HEADS = 8
LAYERS = 2


EPSILON = 1e-05


def padded_2(cells, sides, width):
    for axis, dim in sides:
        count = lax.axis_size(axis)
        ends = count - 1
        head = lax.slice_in_dim(cells, 0, width, axis=dim)
        tail = lax.slice_in_dim(cells, cells.shape[dim] - width, cells.shape[dim], axis=dim)
        cells = jnp.concatenate(
            [
                lax.ppermute(tail, axis, [(i, (i + 1) % count) for i in range(ends)]),
                cells,
                lax.ppermute(head, axis, [((i + 1) % count, i) for i in range(ends)]),
            ],
            axis=dim,
        )
    return cells


def layer_norm(values, gain):
    centre = values - jnp.mean(values, axis=-1, keepdims=True)
    spread = jnp.mean(centre * centre, axis=-1, keepdims=True)
    return centre * lax.rsqrt(spread + EPSILON) * gain


def neighbours(padded):
    parts = [
        padded[1:-1, 1:-1, 1:-1],
        padded[:-2, 1:-1, 1:-1],
        padded[2:, 1:-1, 1:-1],
        padded[1:-1, :-2, 1:-1],
        padded[1:-1, 2:, 1:-1],
        padded[1:-1, 1:-1, :-2],
        padded[1:-1, 1:-1, 2:],
    ]
    return jnp.stack(parts, axis=3)


def attend(query, keys, values, mask, heads):
    batch, slots, width = query.shape
    head_size = width // heads
    total_keys = keys.shape[1]
    query_heads = query.reshape(batch, slots, heads, head_size)
    key_heads = keys.reshape(batch, total_keys, heads, head_size)
    value_heads = values.reshape(batch, total_keys, heads, head_size)
    scores = jnp.einsum(
        "bqhd,bkhd->bhqk", query_heads, key_heads, preferred_element_type=jnp.float32
    ) * head_size ** (-0.5)
    valid = mask[:, None, None, :]
    scores = jnp.where(valid, scores, -1e30)
    peak = jnp.max(scores, axis=-1, keepdims=True)
    weights = jnp.where(valid, jnp.exp(scores - peak), 0.0)
    weights = (weights / jnp.sum(weights, axis=-1, keepdims=True)).astype(jnp.bfloat16)
    mixed = jnp.einsum("bhqk,bkhd->bqhd", weights, value_heads, preferred_element_type=jnp.float32)
    return mixed.astype(jnp.bfloat16).reshape(batch, slots, width)


def update(rows, attended, occupied, out_weight, up_weight, down_weight, attention_gain, feed_gain):
    batch, slots, width = rows.shape
    mixed = jnp.dot(attended.reshape(-1, width), out_weight, preferred_element_type=jnp.float32)
    hidden = layer_norm(rows.reshape(-1, width) + mixed, attention_gain)
    inner = jax.nn.gelu(
        jnp.dot(hidden.astype(jnp.bfloat16), up_weight, preferred_element_type=jnp.float32)
    ).astype(jnp.bfloat16)
    grown = jnp.dot(inner, down_weight, preferred_element_type=jnp.float32)
    result = layer_norm(hidden + grown, feed_gain).reshape(batch, slots, width)
    live = jnp.arange(slots, dtype=jnp.int32)[None, :, None] < occupied[:, None, None]
    return jnp.where(live, result, 0.0)


def project_pair(flat, key_weight, value_weight):
    return jnp.concatenate(
        [
            jnp.dot(flat, key_weight, preferred_element_type=jnp.float32),
            jnp.dot(flat, value_weight, preferred_element_type=jnp.float32),
        ],
        axis=1,
    ).astype(jnp.bfloat16)


def local_layer(
    state,
    counts,
    query_weight,
    key_weight,
    value_weight,
    out_weight,
    up_weight,
    down_weight,
    attention_gain,
    feed_gain,
):
    bins_x, bins_y, bins_z, slots, width = state.shape
    total = bins_x * bins_y * bins_z
    rounded = state.astype(jnp.bfloat16)
    flat = rounded.reshape(-1, width)
    query = (
        jnp.dot(flat, query_weight, preferred_element_type=jnp.float32)
        .astype(jnp.bfloat16)
        .reshape(total, slots, width)
    )
    padded_rows, padded_counts = (
        padded_2(rounded, (("gx", 0), ("gy", 1), ("gz", 2)), 1),
        padded_2(counts, (("gx", 0), ("gy", 1), ("gz", 2)), 1),
    )
    padded = project_pair(padded_rows.reshape(-1, width), key_weight, value_weight)
    padded = padded.reshape(bins_x + 2, bins_y + 2, bins_z + 2, slots, 2 * width)
    keys = neighbours(padded).reshape(total, 7 * slots, 2 * width)
    near = neighbours(padded_counts).reshape(total, 7)
    mask = (jnp.arange(slots, dtype=jnp.int32)[None, None, :] < near[:, :, None]).reshape(
        total, 7 * slots
    )
    groups = max(1, width // 128)
    columns = width // groups
    pieces = []
    for group in range(groups):
        start = group * columns
        pieces.append(
            attend(
                query[..., start : start + columns],
                keys[..., start : start + columns],
                keys[..., width + start : width + start + columns],
                mask,
                HEADS // groups,
            )
        )
    attended = jnp.concatenate(pieces, axis=-1)
    result = update(
        state.reshape(total, slots, width),
        attended,
        counts.reshape(-1),
        out_weight,
        up_weight,
        down_weight,
        attention_gain,
        feed_gain,
    )
    return result.reshape(state.shape)


def relocate(state, counts, dest_bin):
    bins_x, bins_y, bins_z, slots, width = state.shape
    total = bins_x * bins_y * bins_z
    depth = lax.axis_size("gz")
    span_y = bins_y * lax.axis_size("gy")
    span_z = bins_z * depth
    targets = dest_bin.reshape(-1)
    target_z = targets % span_z
    target_y = targets // span_z % span_y
    target_x = targets // (span_z * span_y)
    peer = target_z // bins_z
    local = (target_x % bins_x * bins_y + target_y % bins_y) * bins_z + target_z % bins_z
    order = jnp.arange(total, dtype=jnp.int32)
    earlier = (peer[None, :] == peer[:, None]) & (order[None, :] < order[:, None])
    slot = jnp.sum(earlier.astype(jnp.int32), axis=1)
    capacity = (total + depth - 1) // depth
    outgoing = (
        jnp.zeros((depth, capacity, slots, width), jnp.float32)
        .at[peer, slot]
        .set(state.reshape(total, slots, width))
    )
    outgoing_counts = jnp.zeros((depth, capacity), jnp.int32).at[peer, slot].set(counts.reshape(-1))
    outgoing_places = jnp.full((depth, capacity), total, jnp.int32).at[peer, slot].set(local)
    arrived, arrived_counts, arrived_places = (
        lax.all_to_all(
            outgoing.astype(jnp.bfloat16), "gz", split_axis=0, concat_axis=0, tiled=True
        ).astype(outgoing.dtype),
        lax.all_to_all(outgoing_counts, "gz", split_axis=0, concat_axis=0, tiled=True),
        lax.all_to_all(outgoing_places, "gz", split_axis=0, concat_axis=0, tiled=True),
    )
    places = arrived_places.reshape(-1)
    moved = (
        jnp.zeros((total, slots, width), jnp.float32)
        .at[places]
        .set(arrived.reshape(-1, slots, width), mode="drop")
    )
    moved_counts = (
        jnp.zeros((total,), jnp.int32).at[places].set(arrived_counts.reshape(-1), mode="drop")
    )
    return (moved.reshape(state.shape), moved_counts.reshape(counts.shape))


def shards(
    features,
    occupancy,
    dest_bin,
    query_weight,
    key_weight,
    value_weight,
    out_weight,
    up_weight,
    down_weight,
    attention_gain,
    feed_gain,
):
    state, counts = (features, occupancy)
    for layer in range(LAYERS):
        state = local_layer(
            state,
            counts,
            query_weight,
            key_weight,
            value_weight,
            out_weight,
            up_weight,
            down_weight,
            attention_gain,
            feed_gain,
        )
        if layer + 1 < LAYERS:
            state, counts = relocate(state, counts, dest_bin)
    return state


def solution(mesh):
    placed = (
        P("gx", "gy", "gz", None, None),
        P("gx", "gy", "gz"),
        P("gx", "gy", "gz"),
        P(),
        P(),
        P(),
        P(),
        P(),
        P(),
        P(),
        P(),
    )
    return jax.shard_map(
        shards,
        mesh=mesh,
        in_specs=placed,
        out_specs=P("gx", "gy", "gz", None, None),
        check_vma=False,
    )
```

profile of v0, /device:TPU:1, one launch (start us, length us, event | category | flops | bytes accessed | tf_op | source)
XLA Modules:
  0.0 183.8 jit_solution(14431373011011847939)
XLA Ops:
  0.0 1.0 convert_element_type.75
  1.0 4.0 %collective-permute-start = (bf16[1,2,1,128,256]{4,3,2,1,0:T(8,128)(2,1)S(1)}, bf16[1,2,1,128,256]{4,3,2,1,0:T(8,128)(2,1)S(1)}, u32[]{:S(2)}, u32[]{:S(2)}) collective-permute-start(bf16[1,2,1,128,256]{4,3,2,1,0:T(8,128)(2,1)S(1)} %convert_element_type.75), channel_id=1, source_target_pairs={{0,8},{8,16},{16,24},{1,9},{9,17},{17,25},{2,10},{10,18},{18,26},{... | collective-permute-start | bytes 393224 | tf_op jit(solution)/shard_map/ppermute | solution.py:21
  5.1 1.3 collective-permute-start.1
  6.4 4.0 %collective-permute-start.6 = (s32[1,2,1]{1,2,0:T(1,128)}, s32[1,2,1]{1,2,0:T(1,128)S(1)}, u32[]{:S(2)}, u32[]{:S(2)}) collective-permute-start(s32[1,2,1]{1,2,0:T(1,128)} %param.12), channel_id=1, source_target_pairs={{0,8},{8,16},{16,24},{1,9},{9,17},{17,25},{2,10},{10,18},{18,26},{... | collective-permute-start | bytes 32 | tf_op jit(solution)/shard_map/ppermute | solution.py:21
  10.4 1.3 collective-permute-start.7
  11.7 0.7 and_select_fusion
  12.5 0.7 fusion.127
  13.8 0.6 copy.162
  14.4 3.2 %all-to-all-start = ((s32[2,1,1]{2,1,0:T(1,128)}), s32[2,1,1]{2,1,0:T(1,128)S(1)}, u32[]{:S(2)}, u32[]{:S(2)}) async-start(s32[2,1,1]{2,1,0:T(1,128)} %copy.162), calls=%async_computation | async-start | bytes 2048 | tf_op jit(solution)/shard_map/all_to_all | solution.py:179
  17.6 0.7 iota_compare_fusion
  18.4 0.7 scatter_custom_fusion.1
  19.1 0.7 copy.163
  19.8 0.7 copy.172
  20.5 1.1 convolution_convert_fusion.5
  21.9 3.2 %all-to-all-start.1 = ((s32[2,1,1]{2,1,0:T(1,128)}), s32[2,1,1]{2,1,0:T(1,128)S(1)}, u32[]{:S(2)}, u32[]{:S(2)}) async-start(s32[2,1,1]{2,1,0:T(1,128)} %copy.163), calls=%async_computation.1 | async-start | bytes 2048 | tf_op jit(solution)/shard_map/all_to_all | solution.py:178
  25.3 2.5 %all-to-all-done.1 = s32[2,1,1]{2,1,0:T(1,128)S(1)} async-done(((s32[2,1,1]{2,1,0:T(1,128)}), s32[2,1,1]{2,1,0:T(1,128)S(1)}, u32[]{:S(2)}, u32[]{:S(2)}) %all-to-all-start.1) | async-done | bytes 40 | tf_op jit(solution)/shard_map/all_to_all | solution.py:178
  27.9 0.6 scatter_custom_fusion.2
  28.5 4.0 %collective-permute-start.18 = (s32[1,2,1]{1,2,0:T(1,128)S(1)}, s32[1,2,1]{1,2,0:T(1,128)S(1)}, u32[]{:S(2)}, u32[]{:S(2)}) collective-permute-start(s32[1,2,1]{1,2,0:T(1,128)S(1)} %bitcast.294), channel_id=1, source_target_pairs={{0,8},{8,16},{16,24},{1,9},{9,17},{17,25},{2,10},{10,18},{18,26},{... | collective-permute-start | bytes 32 | tf_op jit(solution)/shard_map/ppermute | solution.py:21
  32.6 1.3 collective-permute-start.19
  33.9 0.7 constant_dynamic-update-slice_fusion.1
  34.6 6.1 %collective-permute-start.8 = (s32[3,1,1]{1,2,0:T(1,128)S(1)}, s32[3,1,1]{1,2,0:T(1,128)S(1)}, u32[]{:S(2)}, u32[]{:S(2)}) collective-permute-start(s32[3,1,1]{1,2,0:T(1,128)S(1)} %get-tuple-element.30), channel_id=1, source_target_pairs={{0,2},{2,4},{4,6},{1,3},{3,5},{5,7},{8,10},{10,12},{12,14},{9,11},... | collective-permute-start | bytes 44 | tf_op jit(solution)/shard_map/ppermute | solution.py:21
  40.9 1.9 %collective-permute-start.9 = (s32[3,1,1]{1,2,0:T(1,128)S(1)}, s32[3,1,1]{1,2,0:T(1,128)S(1)}, u32[]{:S(2)}, u32[]{:S(2)}) collective-permute-start(s32[3,1,1]{1,2,0:T(1,128)S(1)} %get-tuple-element.29), channel_id=1, source_target_pairs={{2,0},{4,2},{6,4},{3,1},{5,3},{7,5},{10,8},{12,10},{14,12},{11,9},... | collective-permute-start | bytes 44 | tf_op jit(solution)/shard_map/ppermute | solution.py:23
  43.0 3.6 %collective-permute-start.20 = (s32[3,1,1]{1,2,0:T(1,128)S(1)}, s32[3,1,1]{1,2,0:T(1,128)S(1)}, u32[]{:S(2)}, u32[]{:S(2)}) collective-permute-start(s32[3,1,1]{1,2,0:T(1,128)S(1)} %get-tuple-element.26), channel_id=1, source_target_pairs={{0,2},{2,4},{4,6},{1,3},{3,5},{5,7},{8,10},{10,12},{12,14},{9,11},... | collective-permute-start | bytes 44 | tf_op jit(solution)/shard_map/ppermute | solution.py:21
  46.8 1.9 %collective-permute-start.21 = (s32[3,1,1]{1,2,0:T(1,128)S(1)}, s32[3,1,1]{1,2,0:T(1,128)S(1)}, u32[]{:S(2)}, u32[]{:S(2)}) collective-permute-start(s32[3,1,1]{1,2,0:T(1,128)S(1)} %get-tuple-element.25), channel_id=1, source_target_pairs={{2,0},{4,2},{6,4},{3,1},{5,3},{7,5},{10,8},{12,10},{14,12},{11,9},... | collective-permute-start | bytes 44 | tf_op jit(solution)/shard_map/ppermute | solution.py:23
  48.8 1.8 collective-permute-start.10
  50.8 1.3 collective-permute-start.11
  52.2 4.0 %collective-permute-start.22 = (s32[3,4,1]{1,2,0:T(1,128)S(1)}, s32[3,4,1]{1,2,0:T(1,128)S(1)}, u32[]{:S(2)}, u32[]{:S(2)}) collective-permute-start(s32[3,4,1]{1,2,0:T(1,128)S(1)} %pad_add_fusion.2), channel_id=1, source_target_pairs={{0,1},{2,3},{4,5},{6,7},{8,9},{10,11},{12,13},{14,15},{16,17},{18,... | collective-permute-start | bytes 152 | tf_op jit(solution)/shard_map/ppermute | solution.py:21
  56.5 1.3 collective-permute-start.23
  58.0 4.5 %collective-permute-start.2 = (bf16[3,1,1,128,256]{4,3,2,1,0:T(8,128)(2,1)S(1)}, bf16[3,1,1,128,256]{4,3,2,1,0:T(8,128)(2,1)S(1)}, u32[]{:S(2)}, u32[]{:S(2)}) collective-permute-start(bf16[3,1,1,128,256]{4,3,2,1,0:T(8,128)(2,1)S(1)} %get-tuple-element.15), channel_id=1, source_target_pairs={{0,2},{2,4},{4,6},{1,3},{3,5},{5,7},{8,10},{10,12},{12,14},{9,11},... | collective-permute-start | bytes 589832 | tf_op jit(solution)/shard_map/ppermute | solution.py:21
  62.5 1.9 %collective-permute-start.3 = (bf16[3,1,1,128,256]{4,3,2,1,0:T(8,128)(2,1)S(1)}, bf16[3,1,1,128,256]{4,3,2,1,0:T(8,128)(2,1)S(1)}, u32[]{:S(2)}, u32[]{:S(2)}) collective-permute-start(bf16[3,1,1,128,256]{4,3,2,1,0:T(8,128)(2,1)S(1)} %get-tuple-element.16), channel_id=1, source_target_pairs={{2,0},{4,2},{6,4},{3,1},{5,3},{7,5},{10,8},{12,10},{14,12},{11,9},... | collective-permute-start | bytes 589832 | tf_op jit(solution)/shard_map/ppermute | solution.py:23
  65.1 4.4 %collective-permute-done.3 = bf16[3,1,1,128,256]{4,3,2,1,0:T(8,128)(2,1)S(1)} collective-permute-done((bf16[3,1,1,128,256]{4,3,2,1,0:T(8,128)(2,1)S(1)}, bf16[3,1,1,128,256]{4,3,2,1,0:T(8,128)(2,1)S(1)}, u32[]{:S(2)}, u32[]{:S(2)}) %collective-permute-start.3) | collective-permute-done | bytes 196640 | tf_op jit(solution)/shard_map/ppermute | solution.py:23
  69.6 5.2 %collective-permute-start.4 = (bf16[3,4,1,128,256]{4,3,2,1,0:T(8,128)(2,1)S(1)}, bf16[3,4,1,128,256]{4,3,2,1,0:T(8,128)(2,1)}, u32[]{:S(2)}, u32[]{:S(2)}) collective-permute-start(bf16[3,4,1,128,256]{4,3,2,1,0:T(8,128)(2,1)S(1)} %pad_maximum_fusion.2), channel_id=1, source_target_pairs={{0,1},{2,3},{4,5},{6,7},{8,9},{10,11},{12,13},{14,15},{16,17},{18,... | collective-permute-start | bytes 2359304 | tf_op jit(solution)/shard_map/ppermute | solution.py:21
  74.8 1.3 collective-permute-start.5
  76.6 11.4 %collective-permute-done.4 = bf16[3,4,1,128,256]{4,3,2,1,0:T(8,128)(2,1)} collective-permute-done((bf16[3,4,1,128,256]{4,3,2,1,0:T(8,128)(2,1)S(1)}, bf16[3,4,1,128,256]{4,3,2,1,0:T(8,128)(2,1)}, u32[]{:S(2)}, u32[]{:S(2)}) %collective-permute-start.4) | collective-permute-done | bytes 786464 | tf_op jit(solution)/shard_map/ppermute | solution.py:21
  88.0 5.1 %collective-permute-done.5 = bf16[3,4,1,128,256]{4,3,2,1,0:T(8,128)(2,1)} collective-permute-done((bf16[3,4,1,128,256]{4,3,2,1,0:T(8,128)(2,1)S(1)}, bf16[3,4,1,128,256]{4,3,2,1,0:T(8,128)(2,1)}, u32[]{:S(2)}, u32[]{:S(2)}) %collective-permute-start.5) | collective-permute-done | bytes 786464 | tf_op jit(solution)/shard_map/ppermute | solution.py:23
  93.1 2.2 %convolution_convert_fusion.3 = bf16[3,4,3,128,256]{4,3,2,1,0:T(8,128)(2,1)S(1)} fusion(bf16[256,256]{1,0:T(8,128)(2,1)S(1)} %copy-done.7, bf16[3,4,1,128,256]{4,3,2,1,0:T(8,128)(2,1)} %collective-permute-done.5, bf16[3,1,1,128,256]{4,3,2,1,0:T(8,128)(2,1)S(1)} %collective-permute-done.3, bf16[1,2,1,128,256]{4,3,2,1,0:T(8,128)(2,1)S(1)} %collective-permute-done.1, ...), kind=kOutput, calls=%fused_computation.30 | convolution fusion | flops 612237312 | bytes 4849664 | tf_op jit(solution)/shard_map/dot_general | solution.py:84
  95.3 2.2 %convolution_convert_fusion.2 = bf16[3,4,3,128,256]{4,3,2,1,0:T(8,128)(2,1)S(1)} fusion(bf16[256,256]{1,0:T(8,128)(2,1)S(1)} %copy-done.8, bf16[3,4,1,128,256]{4,3,2,1,0:T(8,128)(2,1)} %collective-permute-done.5, bf16[3,1,1,128,256]{4,3,2,1,0:T(8,128)(2,1)S(1)} %collective-permute-done.3, bf16[1,2,1,128,256]{4,3,2,1,0:T(8,128)(2,1)S(1)} %collective-permute-done.1, ...), kind=kOutput, calls=%fused_computation.29 | convolution fusion | flops 612237312 | bytes 4849664 | tf_op jit(solution)/shard_map/dot_general | solution.py:85
  98.7 3.3 %fusion.161 = (f32[2,4,128]{2,1,0:T(4,128)S(1)}, f32[2,4,128,896]{3,2,1,0:T(8,128)}) fusion(pred[2,896]{1,0:T(4,128)(4,1)S(1)} %get-tuple-element.22, bf16[2,128,4,32]{1,3,2,0:T(8,128)(2,1)S(1)} %bitcast.291, bf16[2,896,4,32]{1,3,2,0:T(8,128)(2,1)S(1)} %bitcast.281), kind=kOutput, calls=%fused_computation.257 | convolution fusion | flops 63308672 | bytes 4200192 | tf_op jit(solution)/shard_map/sub | solution.py:62
  102.0 2.8 %fusion.28 = bf16[2,128,4,32]{1,3,2,0:T(8,128)(2,1)S(1)} fusion(bf16[2,896,4,32]{1,3,2,0:T(8,128)(2,1)S(1)} %bitcast.279, f32[2,4,128,896]{3,2,1,0:T(8,128)} %get-tuple-element.36, f32[2,4,128]{2,1,0:T(4,128)S(1)} %get-tuple-element.35), kind=kOutput, calls=%fused_computation.59 | convolution fusion | flops 60588032 | bytes 4198400 | tf_op jit(solution)/shard_map/bhqk,bkhd->bqhd/dot_general | solution.py:64
  105.4 3.3 %fusion.160 = (f32[2,4,128]{2,1,0:T(4,128)S(1)}, f32[2,4,128,896]{3,2,1,0:T(8,128)}) fusion(pred[2,896]{1,0:T(4,128)(4,1)S(1)} %get-tuple-element.22, bf16[2,128,4,32]{1,3,2,0:T(8,128)(2,1)S(1)} %bitcast.290, bf16[2,896,4,32]{1,3,2,0:T(8,128)(2,1)S(1)} %bitcast.274), kind=kOutput, calls=%fused_computation.256 | convolution fusion | flops 63308672 | bytes 4200192 | tf_op jit(solution)/shard_map/sub | solution.py:62
  108.7 2.9 %fusion.29 = bf16[2,128,4,32]{1,3,2,0:T(8,128)(2,1)S(1)} fusion(bf16[2,896,4,32]{1,3,2,0:T(8,128)(2,1)S(1)} %bitcast.275, f32[2,4,128,896]{3,2,1,0:T(8,128)} %get-tuple-element.34, f32[2,4,128]{2,1,0:T(4,128)S(1)} %get-tuple-element.33), kind=kOutput, calls=%fused_computation.60 | convolution fusion | flops 60588032 | bytes 4198400 | tf_op jit(solution)/shard_map/bhqk,bkhd->bqhd/dot_general | solution.py:64
  112.3 0.7 fusion.163
  113.6 0.6 scatter_fusion
  114.2 5.7 %all_to_all.26 = bf16[2,1,128,256]{3,2,1,0:T(8,128)(2,1)S(1)} all-to-all(bf16[2,1,128,256]{3,2,1,0:T(8,128)(2,1)S(1)} %convert_bitcast_fusion), channel_id=1, replica_groups=mesh['gx'=4,'gy'=4,'gz'=2] {'gz'}, dimensions={0} | all-to-all | bytes 262144 | tf_op jit(solution)/shard_map/all_to_all | solution.py:175
  120.0 0.6 scatter_fusion.1
  120.6 4.3 %collective-permute-start.12 = (bf16[1,2,1,128,256]{4,3,2,1,0:T(8,128)(2,1)S(1)}, bf16[1,2,1,128,256]{4,3,2,1,0:T(8,128)(2,1)S(1)}, u32[]{:S(2)}, u32[]{:S(2)}) collective-permute-start(bf16[1,2,1,128,256]{4,3,2,1,0:T(8,128)(2,1)S(1)} %convert_bitcast_fusion.1), channel_id=1, source_target_pairs={{0,8},{8,16},{16,24},{1,9},{9,17},{17,25},{2,10},{10,18},{18,26},{... | collective-permute-start | bytes 393224 | tf_op jit(solution)/shard_map/ppermute | solution.py:21
  124.9 1.3 collective-permute-start.13
  126.2 1.4 collective-permute-done.12
  127.6 4.1 %collective-permute-done.13 = bf16[1,2,1,128,256]{4,3,2,1,0:T(8,128)(2,1)S(1)} collective-permute-done((bf16[1,2,1,128,256]{4,3,2,1,0:T(8,128)(2,1)S(1)}, bf16[1,2,1,128,256]{4,3,2,1,0:T(8,128)(2,1)S(1)}, u32[]{:S(2)}, u32[]{:S(2)}) %collective-permute-start.13) | collective-permute-done | bytes 131104 | tf_op jit(solution)/shard_map/ppermute | solution.py:23
  131.8 3.0 %collective-permute-start.14 = (bf16[3,1,1,128,256]{4,3,2,1,0:T(8,128)(2,1)S(1)}, bf16[3,1,1,128,256]{4,3,2,1,0:T(8,128)(2,1)S(1)}, u32[]{:S(2)}, u32[]{:S(2)}) collective-permute-start(bf16[3,1,1,128,256]{4,3,2,1,0:T(8,128)(2,1)S(1)} %get-tuple-element.13), channel_id=1, source_target_pairs={{0,2},{2,4},{4,6},{1,3},{3,5},{5,7},{8,10},{10,12},{12,14},{9,11},... | collective-permute-start | bytes 589832 | tf_op jit(solution)/shard_map/ppermute | solution.py:21
  134.8 2.1 %collective-permute-start.15 = (bf16[3,1,1,128,256]{4,3,2,1,0:T(8,128)(2,1)S(1)}, bf16[3,1,1,128,256]{4,3,2,1,0:T(8,128)(2,1)S(1)}, u32[]{:S(2)}, u32[]{:S(2)}) collective-permute-start(bf16[3,1,1,128,256]{4,3,2,1,0:T(8,128)(2,1)S(1)} %get-tuple-element.14), channel_id=1, source_target_pairs={{2,0},{4,2},{6,4},{3,1},{5,3},{7,5},{10,8},{12,10},{14,12},{11,9},... | collective-permute-start | bytes 589832 | tf_op jit(solution)/shard_map/ppermute | solution.py:23
  137.4 4.4 %collective-permute-done.15 = bf16[3,1,1,128,256]{4,3,2,1,0:T(8,128)(2,1)S(1)} collective-permute-done((bf16[3,1,1,128,256]{4,3,2,1,0:T(8,128)(2,1)S(1)}, bf16[3,1,1,128,256]{4,3,2,1,0:T(8,128)(2,1)S(1)}, u32[]{:S(2)}, u32[]{:S(2)}) %collective-permute-start.15) | collective-permute-done | bytes 196640 | tf_op jit(solution)/shard_map/ppermute | solution.py:23
  141.9 2.6 %collective-permute-start.16 = (bf16[3,4,1,128,256]{4,3,2,1,0:T(8,128)(2,1)S(1)}, bf16[3,4,1,128,256]{4,3,2,1,0:T(8,128)(2,1)}, u32[]{:S(2)}, u32[]{:S(2)}) collective-permute-start(bf16[3,4,1,128,256]{4,3,2,1,0:T(8,128)(2,1)S(1)} %pad_maximum_fusion.3), channel_id=1, source_target_pairs={{0,1},{2,3},{4,5},{6,7},{8,9},{10,11},{12,13},{14,15},{16,17},{18,... | collective-permute-start | bytes 2359304 | tf_op jit(solution)/shard_map/ppermute | solution.py:21
  144.4 1.3 collective-permute-start.17
  146.3 11.4 %collective-permute-done.16 = bf16[3,4,1,128,256]{4,3,2,1,0:T(8,128)(2,1)} collective-permute-done((bf16[3,4,1,128,256]{4,3,2,1,0:T(8,128)(2,1)S(1)}, bf16[3,4,1,128,256]{4,3,2,1,0:T(8,128)(2,1)}, u32[]{:S(2)}, u32[]{:S(2)}) %collective-permute-start.16) | collective-permute-done | bytes 786464 | tf_op jit(solution)/shard_map/ppermute | solution.py:21
  157.7 5.1 %collective-permute-done.17 = bf16[3,4,1,128,256]{4,3,2,1,0:T(8,128)(2,1)} collective-permute-done((bf16[3,4,1,128,256]{4,3,2,1,0:T(8,128)(2,1)S(1)}, bf16[3,4,1,128,256]{4,3,2,1,0:T(8,128)(2,1)}, u32[]{:S(2)}, u32[]{:S(2)}) %collective-permute-start.17) | collective-permute-done | bytes 786464 | tf_op jit(solution)/shard_map/ppermute | solution.py:23
  162.8 2.2 %convolution_convert_fusion.1 = bf16[3,4,3,128,256]{4,3,2,1,0:T(8,128)(2,1)S(1)} fusion(bf16[256,256]{1,0:T(8,128)(2,1)S(1)} %copy-done.7, bf16[3,4,1,128,256]{4,3,2,1,0:T(8,128)(2,1)} %collective-permute-done.17, bf16[3,1,1,128,256]{4,3,2,1,0:T(8,128)(2,1)S(1)} %collective-permute-done.15, bf16[1,2,1,128,256]{4,3,2,1,0:T(8,128)(2,1)S(1)} %collective-permute-done.13, ...), kind=kOutput, calls=%fused_computation.28 | convolution fusion | flops 612237312 | bytes 4849664 | tf_op jit(solution)/shard_map/dot_general | solution.py:84
  165.0 2.2 %convolution_convert_fusion = bf16[3,4,3,128,256]{4,3,2,1,0:T(8,128)(2,1)S(1)} fusion(bf16[256,256]{1,0:T(8,128)(2,1)S(1)} %copy-done.8, bf16[3,4,1,128,256]{4,3,2,1,0:T(8,128)(2,1)} %collective-permute-done.17, bf16[3,1,1,128,256]{4,3,2,1,0:T(8,128)(2,1)S(1)} %collective-permute-done.15, bf16[1,2,1,128,256]{4,3,2,1,0:T(8,128)(2,1)S(1)} %collective-permute-done.13, ...), kind=kOutput, calls=%fused_computation.27 | convolution fusion | flops 612237312 | bytes 4849664 | tf_op jit(solution)/shard_map/dot_general | solution.py:85
  168.4 3.3 %fusion.167 = (f32[2,4,128]{2,1,0:T(4,128)S(1)}, f32[2,4,128,896]{3,2,1,0:T(8,128)}) fusion(pred[2,896]{1,0:T(4,128)(4,1)S(1)} %get-tuple-element.21, bf16[2,128,4,32]{1,3,2,0:T(8,128)(2,1)S(1)} %bitcast.293, bf16[2,896,4,32]{1,3,2,0:T(8,128)(2,1)S(1)} %bitcast.280), kind=kOutput, calls=%fused_computation.261 | convolution fusion | flops 63308672 | bytes 4200192 | tf_op jit(solution)/shard_map/sub | solution.py:62
  171.6 2.8 %fusion.30 = bf16[2,128,4,32]{1,3,2,0:T(8,128)(2,1)S(1)} fusion(bf16[2,896,4,32]{1,3,2,0:T(8,128)(2,1)S(1)} %bitcast.276, f32[2,4,128,896]{3,2,1,0:T(8,128)} %get-tuple-element.44, f32[2,4,128]{2,1,0:T(4,128)S(1)} %get-tuple-element.43), kind=kOutput, calls=%fused_computation.61 | convolution fusion | flops 60588032 | bytes 4198400 | tf_op jit(solution)/shard_map/bhqk,bkhd->bqhd/dot_general | solution.py:64
  175.1 3.3 %fusion.166 = (f32[2,4,128]{2,1,0:T(4,128)S(1)}, f32[2,4,128,896]{3,2,1,0:T(8,128)}) fusion(pred[2,896]{1,0:T(4,128)(4,1)S(1)} %get-tuple-element.21, bf16[2,128,4,32]{1,3,2,0:T(8,128)(2,1)S(1)} %bitcast.292, bf16[2,896,4,32]{1,3,2,0:T(8,128)(2,1)S(1)} %bitcast.277), kind=kOutput, calls=%fused_computation.260 | convolution fusion | flops 63308672 | bytes 4200192 | tf_op jit(solution)/shard_map/sub | solution.py:62
  178.4 2.9 %fusion.31 = bf16[2,128,4,32]{1,3,2,0:T(8,128)(2,1)S(1)} fusion(bf16[2,896,4,32]{1,3,2,0:T(8,128)(2,1)S(1)} %bitcast.278, f32[2,4,128,896]{3,2,1,0:T(8,128)} %get-tuple-element.42, f32[2,4,128]{2,1,0:T(4,128)S(1)} %get-tuple-element.41), kind=kOutput, calls=%fused_computation.62 | convolution fusion | flops 60588032 | bytes 4198400 | tf_op jit(solution)/shard_map/bhqk,bkhd->bqhd/dot_general | solution.py:64
  181.9 0.7 fusion.169
  183.0 0.8 broadcast_select_fusion
  (144 shorter events, 11.0 us)
Async XLA Ops:
  0.0 112.3 %copy-start = (bf16[1024,256]{1,0:T(8,128)(2,1)S(1)}, bf16[1024,256]{1,0:T(8,128)(2,1)}, u32[]{:S(2)}) copy-start(bf16[1024,256]{1,0:T(8,128)(2,1)} %param.19) | copy-start | bytes 1572868
  0.0 93.1 %copy-start.7 = (bf16[256,256]{1,0:T(8,128)(2,1)S(1)}, bf16[256,256]{1,0:T(8,128)(2,1)}, u32[]{:S(2)}) copy-start(bf16[256,256]{1,0:T(8,128)(2,1)} %param.15) | copy-start | bytes 393220
  1.0 56.9 %collective-permute-start = (bf16[1,2,1,128,256]{4,3,2,1,0:T(8,128)(2,1)S(1)}, bf16[1,2,1,128,256]{4,3,2,1,0:T(8,128)(2,1)S(1)}, u32[]{:S(2)}, u32[]{:S(2)}) collective-permute-start(bf16[1,2,1,128,256]{4,3,2,1,0:T(8,128)(2,1)S(1)} %convert_element_type.75), channel_id=1, source_target_pairs={{0,8},{8,16},{16,24},{1,9},{9,17},{17,25},{2,10},{10,18},{18,26},{... | collective-permute-start | bytes 393224 | tf_op jit(solution)/shard_map/ppermute | solution.py:21
  5.1 52.9 %collective-permute-start.1 = (bf16[1,2,1,128,256]{4,3,2,1,0:T(8,128)(2,1)S(1)}, bf16[1,2,1,128,256]{4,3,2,1,0:T(8,128)(2,1)S(1)}, u32[]{:S(2)}, u32[]{:S(2)}) collective-permute-start(bf16[1,2,1,128,256]{4,3,2,1,0:T(8,128)(2,1)S(1)} %convert_element_type.75), channel_id=1, source_target_pairs={{8,0},{16,8},{24,16},{9,1},{17,9},{25,17},{10,2},{18,10},{26,18},{... | collective-permute-start | bytes 393224 | tf_op jit(solution)/shard_map/ppermute | solution.py:23
  6.4 26.2 %collective-permute-start.6 = (s32[1,2,1]{1,2,0:T(1,128)}, s32[1,2,1]{1,2,0:T(1,128)S(1)}, u32[]{:S(2)}, u32[]{:S(2)}) collective-permute-start(s32[1,2,1]{1,2,0:T(1,128)} %param.12), channel_id=1, source_target_pairs={{0,8},{8,16},{16,24},{1,9},{9,17},{17,25},{2,10},{10,18},{18,26},{... | collective-permute-start | bytes 32 | tf_op jit(solution)/shard_map/ppermute | solution.py:21
  10.4 24.2 %collective-permute-start.7 = (s32[1,2,1]{1,2,0:T(1,128)}, s32[1,2,1]{1,2,0:T(1,128)S(1)}, u32[]{:S(2)}, u32[]{:S(2)}) collective-permute-start(s32[1,2,1]{1,2,0:T(1,128)} %param.12), channel_id=1, source_target_pairs={{8,0},{16,8},{24,16},{9,1},{17,9},{25,17},{10,2},{18,10},{26,18},{... | collective-permute-start | bytes 32 | tf_op jit(solution)/shard_map/ppermute | solution.py:23
  14.4 7.5 %all-to-all-start = ((s32[2,1,1]{2,1,0:T(1,128)}), s32[2,1,1]{2,1,0:T(1,128)S(1)}, u32[]{:S(2)}, u32[]{:S(2)}) async-start(s32[2,1,1]{2,1,0:T(1,128)} %copy.162), calls=%async_computation | async-start | bytes 2048 | tf_op jit(solution)/shard_map/all_to_all | solution.py:179
  21.9 5.8 %all-to-all-start.1 = ((s32[2,1,1]{2,1,0:T(1,128)}), s32[2,1,1]{2,1,0:T(1,128)S(1)}, u32[]{:S(2)}, u32[]{:S(2)}) async-start(s32[2,1,1]{2,1,0:T(1,128)} %copy.163), calls=%async_computation.1 | async-start | bytes 2048 | tf_op jit(solution)/shard_map/all_to_all | solution.py:178
  28.5 12.5 %collective-permute-start.18 = (s32[1,2,1]{1,2,0:T(1,128)S(1)}, s32[1,2,1]{1,2,0:T(1,128)S(1)}, u32[]{:S(2)}, u32[]{:S(2)}) collective-permute-start(s32[1,2,1]{1,2,0:T(1,128)S(1)} %bitcast.294), channel_id=1, source_target_pairs={{0,8},{8,16},{16,24},{1,9},{9,17},{17,25},{2,10},{10,18},{18,26},{... | collective-permute-start | bytes 32 | tf_op jit(solution)/shard_map/ppermute | solution.py:21
  32.6 10.3 %collective-permute-start.19 = (s32[1,2,1]{1,2,0:T(1,128)S(1)}, s32[1,2,1]{1,2,0:T(1,128)S(1)}, u32[]{:S(2)}, u32[]{:S(2)}) collective-permute-start(s32[1,2,1]{1,2,0:T(1,128)S(1)} %bitcast.296), channel_id=1, source_target_pairs={{8,0},{16,8},{24,16},{9,1},{17,9},{25,17},{10,2},{18,10},{26,18},{... | collective-permute-start | bytes 32 | tf_op jit(solution)/shard_map/ppermute | solution.py:23
  34.6 12.2 %collective-permute-start.8 = (s32[3,1,1]{1,2,0:T(1,128)S(1)}, s32[3,1,1]{1,2,0:T(1,128)S(1)}, u32[]{:S(2)}, u32[]{:S(2)}) collective-permute-start(s32[3,1,1]{1,2,0:T(1,128)S(1)} %get-tuple-element.30), channel_id=1, source_target_pairs={{0,2},{2,4},{4,6},{1,3},{3,5},{5,7},{8,10},{10,12},{12,14},{9,11},... | collective-permute-start | bytes 44 | tf_op jit(solution)/shard_map/ppermute | solution.py:21
  40.9 7.8 %collective-permute-start.9 = (s32[3,1,1]{1,2,0:T(1,128)S(1)}, s32[3,1,1]{1,2,0:T(1,128)S(1)}, u32[]{:S(2)}, u32[]{:S(2)}) collective-permute-start(s32[3,1,1]{1,2,0:T(1,128)S(1)} %get-tuple-element.29), channel_id=1, source_target_pairs={{2,0},{4,2},{6,4},{3,1},{5,3},{7,5},{10,8},{12,10},{14,12},{11,9},... | collective-permute-start | bytes 44 | tf_op jit(solution)/shard_map/ppermute | solution.py:23
  43.0 7.9 %collective-permute-start.20 = (s32[3,1,1]{1,2,0:T(1,128)S(1)}, s32[3,1,1]{1,2,0:T(1,128)S(1)}, u32[]{:S(2)}, u32[]{:S(2)}) collective-permute-start(s32[3,1,1]{1,2,0:T(1,128)S(1)} %get-tuple-element.26), channel_id=1, source_target_pairs={{0,2},{2,4},{4,6},{1,3},{3,5},{5,7},{8,10},{10,12},{12,14},{9,11},... | collective-permute-start | bytes 44 | tf_op jit(solution)/shard_map/ppermute | solution.py:21
  46.8 5.3 %collective-permute-start.21 = (s32[3,1,1]{1,2,0:T(1,128)S(1)}, s32[3,1,1]{1,2,0:T(1,128)S(1)}, u32[]{:S(2)}, u32[]{:S(2)}) collective-permute-start(s32[3,1,1]{1,2,0:T(1,128)S(1)} %get-tuple-element.25), channel_id=1, source_target_pairs={{2,0},{4,2},{6,4},{3,1},{5,3},{7,5},{10,8},{12,10},{14,12},{11,9},... | collective-permute-start | bytes 44 | tf_op jit(solution)/shard_map/ppermute | solution.py:23
  48.8 7.7 %collective-permute-start.10 = (s32[3,4,1]{1,2,0:T(1,128)S(1)}, s32[3,4,1]{1,2,0:T(1,128)S(1)}, u32[]{:S(2)}, u32[]{:S(2)}) collective-permute-start(s32[3,4,1]{1,2,0:T(1,128)S(1)} %pad_add_fusion), channel_id=1, source_target_pairs={{0,1},{2,3},{4,5},{6,7},{8,9},{10,11},{12,13},{14,15},{16,17},{18,... | collective-permute-start | bytes 152 | tf_op jit(solution)/shard_map/ppermute | solution.py:21
  50.8 13.6 %collective-permute-start.11 = (s32[3,4,1]{1,2,0:T(1,128)S(1)}, s32[3,4,1]{1,2,0:T(1,128)S(1)}, u32[]{:S(2)}, u32[]{:S(2)}) collective-permute-start(s32[3,4,1]{1,2,0:T(1,128)S(1)} %pad_add_fusion), channel_id=1, source_target_pairs={{1,0},{3,2},{5,4},{7,6},{9,8},{11,10},{13,12},{15,14},{17,16},{19,... | collective-permute-start | bytes 152 | tf_op jit(solution)/shard_map/ppermute | solution.py:23
  52.2 23.9 %collective-permute-start.22 = (s32[3,4,1]{1,2,0:T(1,128)S(1)}, s32[3,4,1]{1,2,0:T(1,128)S(1)}, u32[]{:S(2)}, u32[]{:S(2)}) collective-permute-start(s32[3,4,1]{1,2,0:T(1,128)S(1)} %pad_add_fusion.2), channel_id=1, source_target_pairs={{0,1},{2,3},{4,5},{6,7},{8,9},{10,11},{12,13},{14,15},{16,17},{18,... | collective-permute-start | bytes 152 | tf_op jit(solution)/shard_map/ppermute | solution.py:21
  56.5 19.8 %collective-permute-start.23 = (s32[3,4,1]{1,2,0:T(1,128)S(1)}, s32[3,4,1]{1,2,0:T(1,128)S(1)}, u32[]{:S(2)}, u32[]{:S(2)}) collective-permute-start(s32[3,4,1]{1,2,0:T(1,128)S(1)} %pad_add_fusion.2), channel_id=1, source_target_pairs={{1,0},{3,2},{5,4},{7,6},{9,8},{11,10},{13,12},{15,14},{17,16},{19,... | collective-permute-start | bytes 152 | tf_op jit(solution)/shard_map/ppermute | solution.py:23
  58.0 7.1 %collective-permute-start.2 = (bf16[3,1,1,128,256]{4,3,2,1,0:T(8,128)(2,1)S(1)}, bf16[3,1,1,128,256]{4,3,2,1,0:T(8,128)(2,1)S(1)}, u32[]{:S(2)}, u32[]{:S(2)}) collective-permute-start(bf16[3,1,1,128,256]{4,3,2,1,0:T(8,128)(2,1)S(1)} %get-tuple-element.15), channel_id=1, source_target_pairs={{0,2},{2,4},{4,6},{1,3},{3,5},{5,7},{8,10},{10,12},{12,14},{9,11},... | collective-permute-start | bytes 589832 | tf_op jit(solution)/shard_map/ppermute | solution.py:21
  62.5 7.0 %collective-permute-start.3 = (bf16[3,1,1,128,256]{4,3,2,1,0:T(8,128)(2,1)S(1)}, bf16[3,1,1,128,256]{4,3,2,1,0:T(8,128)(2,1)S(1)}, u32[]{:S(2)}, u32[]{:S(2)}) collective-permute-start(bf16[3,1,1,128,256]{4,3,2,1,0:T(8,128)(2,1)S(1)} %get-tuple-element.16), channel_id=1, source_target_pairs={{2,0},{4,2},{6,4},{3,1},{5,3},{7,5},{10,8},{12,10},{14,12},{11,9},... | collective-permute-start | bytes 589832 | tf_op jit(solution)/shard_map/ppermute | solution.py:23
  69.6 18.4 %collective-permute-start.4 = (bf16[3,4,1,128,256]{4,3,2,1,0:T(8,128)(2,1)S(1)}, bf16[3,4,1,128,256]{4,3,2,1,0:T(8,128)(2,1)}, u32[]{:S(2)}, u32[]{:S(2)}) collective-permute-start(bf16[3,4,1,128,256]{4,3,2,1,0:T(8,128)(2,1)S(1)} %pad_maximum_fusion.2), channel_id=1, source_target_pairs={{0,1},{2,3},{4,5},{6,7},{8,9},{10,11},{12,13},{14,15},{16,17},{18,... | collective-permute-start | bytes 2359304 | tf_op jit(solution)/shard_map/ppermute | solution.py:21
  74.8 18.4 %collective-permute-start.5 = (bf16[3,4,1,128,256]{4,3,2,1,0:T(8,128)(2,1)S(1)}, bf16[3,4,1,128,256]{4,3,2,1,0:T(8,128)(2,1)}, u32[]{:S(2)}, u32[]{:S(2)}) collective-permute-start(bf16[3,4,1,128,256]{4,3,2,1,0:T(8,128)(2,1)S(1)} %pad_maximum_fusion.2), channel_id=1, source_target_pairs={{1,0},{3,2},{5,4},{7,6},{9,8},{11,10},{13,12},{15,14},{17,16},{19,... | collective-permute-start | bytes 2359304 | tf_op jit(solution)/shard_map/ppermute | solution.py:23
  76.6 18.7 %copy-start.8 = (bf16[256,256]{1,0:T(8,128)(2,1)S(1)}, bf16[256,256]{1,0:T(8,128)(2,1)}, u32[]{:S(2)}) copy-start(bf16[256,256]{1,0:T(8,128)(2,1)} %param.16) | copy-start | bytes 393220
  108.7 3.1 %copy-start.1 = (f32[1,2,1,128,256]{4,3,2,1,0:T(8,128)S(1)}, f32[1,2,1,128,256]{4,3,2,1,0:T(8,128)}, u32[]{:S(2)}) copy-start(f32[1,2,1,128,256]{4,3,2,1,0:T(8,128)} %param.11) | copy-start | bytes 786436
  108.7 3.1 %copy-start.3 = (bf16[256,256]{1,0:T(8,128)(2,1)S(1)}, bf16[256,256]{1,0:T(8,128)(2,1)}, u32[]{:S(2)}) copy-start(bf16[256,256]{1,0:T(8,128)(2,1)} %param.17) | copy-start | bytes 393220
  108.7 3.6 %copy-start.5 = (bf16[256,1024]{1,0:T(8,128)(2,1)S(1)}, bf16[256,1024]{1,0:T(8,128)(2,1)}, u32[]{:S(2)}) copy-start(bf16[256,1024]{1,0:T(8,128)(2,1)} %param.18) | copy-start | bytes 1572868
  108.7 3.6 %copy-start.9 = (f32[256]{0:T(256)S(1)}, f32[256]{0:T(256)}, u32[]{:S(2)}) copy-start(f32[256]{0:T(256)} %param.20) | copy-start | bytes 3076
  112.1 1.2 copy-start.4
  120.0 25.9 %copy-start.2 = (bf16[256,256]{1,0:T(8,128)(2,1)S(1)}, bf16[256,256]{1,0:T(8,128)(2,1)}, u32[]{:S(2)}) copy-start(bf16[256,256]{1,0:T(8,128)(2,1)} %param.14) | copy-start | bytes 393220
  120.6 7.0 %collective-permute-start.12 = (bf16[1,2,1,128,256]{4,3,2,1,0:T(8,128)(2,1)S(1)}, bf16[1,2,1,128,256]{4,3,2,1,0:T(8,128)(2,1)S(1)}, u32[]{:S(2)}, u32[]{:S(2)}) collective-permute-start(bf16[1,2,1,128,256]{4,3,2,1,0:T(8,128)(2,1)S(1)} %convert_bitcast_fusion.1), channel_id=1, source_target_pairs={{0,8},{8,16},{16,24},{1,9},{9,17},{17,25},{2,10},{10,18},{18,26},{... | collective-permute-start | bytes 393224 | tf_op jit(solution)/shard_map/ppermute | solution.py:21
  124.9 6.8 %collective-permute-start.13 = (bf16[1,2,1,128,256]{4,3,2,1,0:T(8,128)(2,1)S(1)}, bf16[1,2,1,128,256]{4,3,2,1,0:T(8,128)(2,1)S(1)}, u32[]{:S(2)}, u32[]{:S(2)}) collective-permute-start(bf16[1,2,1,128,256]{4,3,2,1,0:T(8,128)(2,1)S(1)} %convert_bitcast_fusion.1), channel_id=1, source_target_pairs={{8,0},{16,8},{24,16},{9,1},{17,9},{25,17},{10,2},{18,10},{26,18},{... | collective-permute-start | bytes 393224 | tf_op jit(solution)/shard_map/ppermute | solution.py:23
  131.8 5.6 %collective-permute-start.14 = (bf16[3,1,1,128,256]{4,3,2,1,0:T(8,128)(2,1)S(1)}, bf16[3,1,1,128,256]{4,3,2,1,0:T(8,128)(2,1)S(1)}, u32[]{:S(2)}, u32[]{:S(2)}) collective-permute-start(bf16[3,1,1,128,256]{4,3,2,1,0:T(8,128)(2,1)S(1)} %get-tuple-element.13), channel_id=1, source_target_pairs={{0,2},{2,4},{4,6},{1,3},{3,5},{5,7},{8,10},{10,12},{12,14},{9,11},... | collective-permute-start | bytes 589832 | tf_op jit(solution)/shard_map/ppermute | solution.py:21
  134.8 7.0 %collective-permute-start.15 = (bf16[3,1,1,128,256]{4,3,2,1,0:T(8,128)(2,1)S(1)}, bf16[3,1,1,128,256]{4,3,2,1,0:T(8,128)(2,1)S(1)}, u32[]{:S(2)}, u32[]{:S(2)}) collective-permute-start(bf16[3,1,1,128,256]{4,3,2,1,0:T(8,128)(2,1)S(1)} %get-tuple-element.14), channel_id=1, source_target_pairs={{2,0},{4,2},{6,4},{3,1},{5,3},{7,5},{10,8},{12,10},{14,12},{11,9},... | collective-permute-start | bytes 589832 | tf_op jit(solution)/shard_map/ppermute | solution.py:23
  141.9 15.8 %collective-permute-start.16 = (bf16[3,4,1,128,256]{4,3,2,1,0:T(8,128)(2,1)S(1)}, bf16[3,4,1,128,256]{4,3,2,1,0:T(8,128)(2,1)}, u32[]{:S(2)}, u32[]{:S(2)}) collective-permute-start(bf16[3,4,1,128,256]{4,3,2,1,0:T(8,128)(2,1)S(1)} %pad_maximum_fusion.3), channel_id=1, source_target_pairs={{0,1},{2,3},{4,5},{6,7},{8,9},{10,11},{12,13},{14,15},{16,17},{18,... | collective-permute-start | bytes 2359304 | tf_op jit(solution)/shard_map/ppermute | solution.py:21
  144.4 18.4 %collective-permute-start.17 = (bf16[3,4,1,128,256]{4,3,2,1,0:T(8,128)(2,1)S(1)}, bf16[3,4,1,128,256]{4,3,2,1,0:T(8,128)(2,1)}, u32[]{:S(2)}, u32[]{:S(2)}) collective-permute-start(bf16[3,4,1,128,256]{4,3,2,1,0:T(8,128)(2,1)S(1)} %pad_maximum_fusion.3), channel_id=1, source_target_pairs={{1,0},{3,2},{5,4},{7,6},{9,8},{11,10},{13,12},{15,14},{17,16},{19,... | collective-permute-start | bytes 2359304 | tf_op jit(solution)/shard_map/ppermute | solution.py:23
  178.4 3.5 %copy-start.6 = (bf16[256,1024]{1,0:T(8,128)(2,1)S(1)}, bf16[256,1024]{1,0:T(8,128)(2,1)}, u32[]{:S(2)}) copy-start(bf16[256,1024]{1,0:T(8,128)(2,1)} %param.18) | copy-start | bytes 1572868
where the time goes:
time: 185 us; the launch traced here: 184 us
  starting transfers between devices  71.5 us (39%)
  waiting for transfers between devices  50.7 us (27%)
  matrix products  36.5 us (20%)
  local copies, waits for them, and re-layouts  11.9 us (6%)
  other arithmetic  6.54 us (4%)
  blocking collectives  5.7 us (3%)
    ppermute x12, starting transfers between devices, padded_2(): lax.ppermute(tail, axis, [(i, (i + 1) % count) for i in range(ends)])  47 us
    ppermute x12, waiting for transfers between devices, padded_2(): lax.ppermute(tail, axis, [(i, (i + 1) % count) for i in range(ends)])  25.1 us
    ppermute x12, waiting for transfers between devices, padded_2(): lax.ppermute(head, axis, [((i + 1) % count, i) for i in range(ends)])  23.1 us
    ppermute x12, starting transfers between devices, padded_2(): lax.ppermute(head, axis, [((i + 1) % count, i) for i in range(ends)])  18.1 us
    sub x4, matrix products, attend(): weights = jnp.where(valid, jnp.exp(scores - peak), 0.0)  13 us
    dot_general x4, matrix products, attend(): jnp.einsum('bhqk,bkhd->bqhd', weights, value_heads, preferred_element_typ...  11.5 us
    all_to_all x1, blocking collectives, relocate(): lax.all_to_all(outgoing.astype(jnp.bfloat16), 'gz', split_axis=0, concat_...  5.7 us
    dot_general x2, matrix products, project_pair(): jnp.dot(flat, value_weight, preferred_element_type=jnp.float32)  4.32 us
  transfers between devices with their start and end apart: 26, of which 11 were waited for; matrix products, arithmetic and copies ran while one was open for 6% of the time, Pallas kernels for 0%

commit v1 on v0

v1 whole, which is shorter than its diff:
```python
import functools

import jax
import jax.numpy as jnp
from jax import lax
from jax.experimental import pallas as pl
from jax.experimental.pallas import tpu as pltpu
from jax.sharding import PartitionSpec as P

HEADS = 8
LAYERS = 2
EPSILON = 1e-05
LOG2E = 1.4426950408889634
DEAD = -1e30
HEAD_ROWS = 16

F32 = jnp.float32
BF16 = jnp.bfloat16

VMEM = pl.BlockSpec(memory_space=pltpu.VMEM)
SMEM = pl.BlockSpec(memory_space=pltpu.SMEM)


def call(body, outs, specs, name, limit=24 << 20):
    return pl.pallas_call(
        body,
        out_shape=outs,
        in_specs=specs,
        out_specs=jax.tree.map(lambda _: VMEM, outs),
        compiler_params=pltpu.CompilerParams(vmem_limit_bytes=limit),
        name=name,
    )


def swaps(count, parity):
    pairs = []
    for low in range(parity, count - 1, 2):
        pairs += [(low, low + 1), (low + 1, low)]
    return pairs


def dot(a, b):
    return jnp.dot(a, b, preferred_element_type=F32)


def layer_norm(values, gain):
    centre = values - jnp.mean(values, axis=-1, keepdims=True)
    spread = jnp.mean(centre * centre, axis=-1, keepdims=True)
    return centre * lax.rsqrt(spread + EPSILON) * gain


def header(count, role, width):
    row = lax.broadcasted_iota(jnp.int32, (HEAD_ROWS, width), 0)
    return jnp.where(row == 1, role, count).astype(F32).astype(BF16)


def live_rows(block, slots):
    count = block[slots : slots + 1, :128].astype(F32)
    row = lax.broadcasted_iota(jnp.int32, (slots, 128), 0).astype(F32)
    return row < count


def pack_body(features, counts, both, first, second):
    slots, width = features.shape[1:]
    parity = lax.axis_index("gy") % 2
    for role, single in ((0, first), (1, second)):
        held = 1 - parity if role == 0 else parity
        rows = features[held].astype(BF16)
        top = header(counts[held], role, width)
        both[role, :slots] = rows
        both[role, slots:] = top
        single[:slots] = rows
        single[slots:] = top


def pack(features, counts):
    bins, slots, width = features.shape
    tall = slots + HEAD_ROWS
    outs = [
        jax.ShapeDtypeStruct((bins, tall, width), BF16),
        jax.ShapeDtypeStruct((tall, width), BF16),
        jax.ShapeDtypeStruct((tall, width), BF16),
    ]
    return call(pack_body, outs, [VMEM, SMEM], "pack")(features, counts)


def layer_body(kind, spans, refs, outs):
    (residual, own, halos, sides, weights, gains, extra) = refs
    (query_weight, key_weight, value_weight, out_weight, up_weight, down_weight) = weights
    slots, width = residual.shape[1:]
    head_size = width // HEADS
    groups = width // 128
    per_group = HEADS // groups
    parity = lax.axis_index("gy") % 2
    factor = head_size ** (-0.5) * LOG2E

    flat_rows = []
    lives = []
    for block in (own[0], own[1]):
        flat_rows.append(block[:slots])
        lives.append(live_rows(block, slots))
    for role in range(2):
        for halo in halos:
            block = halo[role]
            flat_rows.append(block[:slots])
            lives.append(live_rows(block, slots))
        block = sides[role][...]
        flat_rows.append(block[:slots])
        lives.append(live_rows(block, slots))
    every = jnp.concatenate(flat_rows, axis=0)
    keys = dot(every, key_weight[...]).astype(BF16)
    values = dot(every, value_weight[...]).astype(BF16)
    queries = dot(jnp.concatenate(flat_rows[:2], axis=0), query_weight[...]).astype(BF16)
    near = len(halos) + 1
    lane = lax.broadcasted_iota(jnp.int32, (slots, 128), 1)
    mark = jnp.where(lane == 0, 1.0, 0.0).astype(BF16)

    attended = []
    for role in range(2):
        picks = [0, 1] + [2 + role * near + n for n in range(near)]

        def gather(array, column, span):
            return jnp.concatenate(
                [array[p * slots : (p + 1) * slots, column : column + span] for p in picks], axis=0
            )

        bias = jnp.concatenate(
            [jnp.where(lives[p], 0.0, DEAD).astype(BF16) for p in picks], axis=0
        )
        mine = gather(values, 0, width)
        query = queries[role * slots : (role + 1) * slots]
        total = None
        for group in range(groups):
            key = jnp.concatenate([gather(keys, group * 128, 128), bias], axis=1)
            for inner in range(per_group):
                head = group * per_group + inner
                inside = (lane >= inner * head_size) & (lane < (inner + 1) * head_size)
                part = query[:, group * 128 : (group + 1) * 128]
                part = jnp.where(inside, part.astype(F32), 0.0).astype(BF16)
                scores = lax.dot_general(
                    jnp.concatenate([part, mark], axis=1),
                    key,
                    (((1,), (1,)), ((), ())),
                    preferred_element_type=F32,
                )
                peak = jnp.max(scores, axis=-1, keepdims=True)
                power = jnp.exp2((scores - peak) * factor)
                scale = 1.0 / jnp.sum(power, axis=-1, keepdims=True)
                mixed = dot((power * scale).astype(BF16), mine)
                column = lax.broadcasted_iota(jnp.int32, (slots, width), 1)
                inside = (column >= head * head_size) & (column < (head + 1) * head_size)
                mixed = jnp.where(inside, mixed, 0.0)
                total = mixed if total is None else total + mixed
        attended.append(total.astype(BF16))
    attended = jnp.concatenate(attended, axis=0)

    attention_gain, feed_gain = gains
    if kind == "features":
        rows = jnp.concatenate([residual[1 - parity], residual[parity]], axis=0)
    else:
        rows = jnp.concatenate([residual[0], residual[1]], axis=0)
    hidden = layer_norm(rows + dot(attended, out_weight[...]), attention_gain[...])
    inner = jax.nn.gelu(dot(hidden.astype(BF16), up_weight[...])).astype(BF16)
    result = layer_norm(hidden + dot(inner, down_weight[...]), feed_gain[...])
    row = lax.broadcasted_iota(jnp.int32, (slots, width), 0).astype(F32)
    results = []
    for role in range(2):
        count = own[role, slots : slots + 1, :].astype(F32)
        results.append(
            jnp.where(row < count, result[role * slots : (role + 1) * slots], 0.0)
        )

    if outs[0] == "bins":
        (out,) = outs[1:]
        out[1 - parity] = results[0]
        out[parity] = results[1]
        return
    travel, stayed = outs[1:]
    places = extra
    span_y, span_z = spans
    for role in range(2):
        held = 1 - parity if role == 0 else parity
        place = places[held]
        stays = place % span_z == lax.axis_index("gz")
        target = (place // span_z) % 2
        new_role = jnp.where(target == parity, 1, 0)
        slot = jnp.where(stays, 1, 0)
        travel[slot, :slots] = results[role].astype(BF16)
        top = own[role, slots:].astype(F32)
        line = lax.broadcasted_iota(jnp.int32, (HEAD_ROWS, width), 0)
        travel[slot, slots:] = jnp.where(line == 1, new_role.astype(F32), top).astype(BF16)

        @pl.when(stays)
        def _():
            stayed[...] = results[role]


def run_layer(kind, end, spans, residual, own, halos, sides, weights, gains, places=None):
    bins, slots, width = residual.shape
    tall = slots + HEAD_ROWS
    n_halo = len(halos)
    if end == "bins":
        outs = [jax.ShapeDtypeStruct((bins, slots, width), F32)]
    else:
        outs = [
            jax.ShapeDtypeStruct((bins, tall, width), BF16),
            jax.ShapeDtypeStruct((slots, width), F32),
        ]
    args = [residual, own, *halos, *sides, *weights, *gains]
    specs = [VMEM] * len(args)
    if end != "bins":
        args.append(places)
        specs.append(SMEM)

    def body(*refs):
        ins, results = refs[: len(args)], refs[len(args) :]
        at = 2 + n_halo
        layer_body(
            kind,
            spans,
            (
                ins[0],
                ins[1],
                ins[2:at],
                ins[at : at + 2],
                ins[at + 2 : at + 8],
                ins[at + 8 : at + 10],
                ins[at + 10] if end != "bins" else None,
            ),
            (end, *results),
        )

    return call(body, outs, specs, f"layer_{kind}_{end}")(*args)


def choose(role, yes, no):
    return jnp.where(role < 0.5, yes.astype(F32), no.astype(F32))


def settle_body(travel, arrived, stayed, both, first, second, beside, residual):
    slots, width = stayed.shape
    stay, came = travel[1], arrived[0]
    role = stay[slots + 1 : slots + 2].astype(F32)
    for index, single in ((0, first), (1, second)):
        block = choose(role, *((stay, came) if index == 0 else (came, stay))).astype(BF16)
        both[index] = block
        single[...] = block
        rows = stayed[...], came[:slots]
        residual[index] = choose(role, *(rows if index == 0 else rows[::-1]))
    peer, left = arrived[1], travel[0]
    role = peer[slots + 1 : slots + 2].astype(F32)
    beside[0] = choose(role, peer, left).astype(BF16)
    beside[1] = choose(role, left, peer).astype(BF16)


def settle(travel, arrived, stayed):
    bins, tall, width = travel.shape
    slots = stayed.shape[0]
    outs = [
        jax.ShapeDtypeStruct((bins, tall, width), BF16),
        jax.ShapeDtypeStruct((tall, width), BF16),
        jax.ShapeDtypeStruct((tall, width), BF16),
        jax.ShapeDtypeStruct((bins, tall, width), BF16),
        jax.ShapeDtypeStruct((bins, slots, width), F32),
    ]
    return call(settle_body, outs, [VMEM] * 3, "settle")(travel, arrived, stayed)


def relocate(state, counts, dest_bin, bins_y):
    total, slots, width = state.shape
    depth = lax.axis_size("gz")
    targets = dest_bin.reshape(-1)
    peer = targets % depth
    local = targets // depth % bins_y
    order = jnp.arange(total, dtype=jnp.int32)
    earlier = (peer[None, :] == peer[:, None]) & (order[None, :] < order[:, None])
    slot = jnp.sum(earlier.astype(jnp.int32), axis=1)
    capacity = (total + depth - 1) // depth
    outgoing = jnp.zeros((depth, capacity, slots, width), F32).at[peer, slot].set(state)
    outgoing_counts = jnp.zeros((depth, capacity), jnp.int32).at[peer, slot].set(counts)
    outgoing_places = jnp.full((depth, capacity), total, jnp.int32).at[peer, slot].set(local)
    arrived = lax.all_to_all(outgoing.astype(BF16), "gz", 0, 0, tiled=True).astype(F32)
    arrived_counts = lax.all_to_all(outgoing_counts, "gz", 0, 0, tiled=True)
    places = lax.all_to_all(outgoing_places, "gz", 0, 0, tiled=True).reshape(-1)
    moved = jnp.zeros((total, slots, width), F32)
    moved = moved.at[places].set(arrived.reshape(-1, slots, width), mode="drop")
    moved_counts = jnp.zeros((total,), jnp.int32)
    moved_counts = moved_counts.at[places].set(arrived_counts.reshape(-1), mode="drop")
    return moved, moved_counts


def line_halo(block, axis):
    count = lax.axis_size(axis)
    return [lax.ppermute(block, axis, swaps(count, p)) for p in range(2) if swaps(count, p)]


def shards(features, occupancy, dest_bin, *rest):
    weights, gains = rest[:6], tuple(g.reshape(1, -1) for g in rest[6:])
    shape = features.shape
    slots, width = shape[3:]
    state = features.reshape(2, slots, width)
    counts = occupancy.reshape(2)
    places = dest_bin.reshape(2)
    depth = lax.axis_size("gz")
    spans = (2 * lax.axis_size("gy"), depth)
    side = lax.axis_size("gy")

    def sideways(first, second):
        return [
            lax.ppermute(block, "gy", swaps(side, p)) for p, block in ((0, first), (1, second))
        ]

    own, first, second = pack(state, counts)
    halos = line_halo(own, "gx") + line_halo(own, "gz")
    sides = sideways(first, second)
    if depth == 2:
        travel, stayed = run_layer(
            "features", "travel", spans, state, own, halos, sides, weights, gains, places
        )
        arrived = lax.ppermute(travel, "gz", swaps(depth, 0))
        own, first, second, beside, residual = settle(travel, arrived, stayed)
        halos = line_halo(own, "gx") + [beside]
        sides = sideways(first, second)
        (out,) = run_layer(
            "settled", "bins", spans, residual, own, halos, sides, weights, gains
        )
    else:
        (state,) = run_layer(
            "features", "bins", spans, state, own, halos, sides, weights, gains
        )
        state, counts = relocate(state, counts, places, 2)
        own, first, second = pack(state, counts)
        halos = line_halo(own, "gx") + line_halo(own, "gz")
        sides = sideways(first, second)
        (out,) = run_layer(
            "features", "bins", spans, state, own, halos, sides, weights, gains
        )
    return out.reshape(shape)


def solution(mesh):
    placed = (
        P("gx", "gy", "gz", None, None),
        P("gx", "gy", "gz"),
        P("gx", "gy", "gz"),
        *([P()] * 8),
    )
    return jax.shard_map(
        shards,
        mesh=mesh,
        in_specs=placed,
        out_specs=P("gx", "gy", "gz", None, None),
        check_vma=False,
    )
```

time: 185 us -> 54.7 us (0.30)
  starting transfers between devices: 71.5 us -> 18.3 us
  waiting for transfers between devices: 50.7 us -> 9.7 us
  matrix products: 36.5 us -> 0 us
  Pallas kernels: 0 us -> 20 us
  other arithmetic: 6.54 us -> 0 us
  local copies, waits for them, and re-layouts: 11.9 us -> 6.17 us
  blocking collectives: 5.7 us -> 0 us
    ppermute x24 -> x10, starting transfers between devices: 65.1 us -> 18.3 us  [the longest x5 10.2 us: line_halo(): lax.ppermute(block, axis, swaps(count, p))]
    ppermute x24 -> x10, waiting for transfers between devices: 48.2 us -> 9.7 us  [the longest x4 5.92 us: sideways(): lax.ppermute(block, 'gy', swaps(side, p))]
    dot_general x14 -> x0, matrix products: 23.5 us -> none  [the longest x4 11.5 us: attend(): jnp.einsum('bhqk,bkhd->bqhd', weights, value_heads, preferred_element_typ...]
    pallas_call x0 -> x4, Pallas kernels: none -> 20 us  [the longest x2 19.4 us: run_layer(): return call(body, outs, specs, f'layer_{kind}_{end}')(*args)]
    sub x4 -> x0, matrix products: 13 us -> none  [attend(): weights = jnp.where(valid, jnp.exp(scores - peak), 0.0)]
    all_to_all x2 -> x0, starting transfers between devices: 6.42 us -> none  [the longest x1 3.23 us: relocate(): lax.all_to_all(outgoing_counts, 'gz', split_axis=0, concat_axis=0, tiled=...]
    all_to_all x1 -> x0, blocking collectives: 5.7 us -> none  [relocate(): lax.all_to_all(outgoing.astype(jnp.bfloat16), 'gz', split_axis=0, concat_...]
    unnamed x27 -> x28, local copies, waits for them, and re-layouts: 0.83 us -> 6.17 us
  transfers between devices with their start and end apart: 26 -> 10, of which waited for: 11 -> 3; matrix products, arithmetic and copies ran while one was open for 6% -> 0% of each run, Pallas kernels for 0% -> 0%
where the time goes in v1:
time: 54.7 us; the launch traced here: 54.4 us
  Pallas kernels  20 us (37%)
  starting transfers between devices  18.3 us (33%)
  waiting for transfers between devices  9.7 us (18%)
  local copies, waits for them, and re-layouts  6.17 us (11%)
    pallas_call x2, Pallas kernels, run_layer(): return call(body, outs, specs, f'layer_{kind}_{end}')(*args)  19.4 us
    ppermute x5, starting transfers between devices, line_halo(): lax.ppermute(block, axis, swaps(count, p))  10.2 us
    ppermute x4, starting transfers between devices, sideways(): lax.ppermute(block, 'gy', swaps(side, p))  7.84 us
    unnamed x28, local copies, waits for them, and re-layouts  6.17 us
    ppermute x4, waiting for transfers between devices, sideways(): lax.ppermute(block, 'gy', swaps(side, p))  5.92 us
    ppermute x1, waiting for transfers between devices, shards(): arrived = lax.ppermute(travel, 'gz', swaps(depth, 0))  3.77 us
  transfers between devices with their start and end apart: 10, of which 3 were waited for; matrix products, arithmetic and copies ran while one was open for 0% of the time, Pallas kernels for 0%

profile of v1, /device:TPU:1, one launch (start us, length us, event | category | flops | bytes accessed | tf_op | source)
XLA Modules:
  0.0 54.4 jit_solution(8264286560458181527)
XLA Ops:
  0.0 0.0 copy-start.12
  0.0 0.7 %copy-done.12 = s32[1,2,1]{1,2,0:T(1,128)S(1)} copy-done((s32[1,2,1]{1,2,0:T(1,128)S(1)}, s32[1,2,1]{1,2,0:T(1,128)}, u32[]{:S(2)}) %copy-start.12) | copy-done | bytes 32
  0.7 0.0 copy-start.4
  0.7 0.9 %copy-done.4 = f32[1,2,1,128,256]{4,3,2,1,0:T(8,128)S(1)} copy-done((f32[1,2,1,128,256]{4,3,2,1,0:T(8,128)S(1)}, f32[1,2,1,128,256]{4,3,2,1,0:T(8,128)}, u32[]{:S(2)}) %copy-start.4) | copy-done | bytes 262168
  1.6 0.0 copy-start.5
  1.6 0.0 copy-start.6
  1.6 0.6 %pack.1 = (bf16[2,144,256]{2,1,0:T(8,128)(2,1)S(1)}, bf16[144,256]{1,0:T(8,128)(2,1)S(1)}, bf16[144,256]{1,0:T(8,128)(2,1)S(1)}) custom-call(f32[2,128,256]{2,1,0:T(8,128)S(1)} %bitcast.8, s32[2]{0:T(128)S(1)} %bitcast.14), custom_call_target="tpu_custom_call" | custom-call | tf_op jit(solution)/shard_map/pack/pallas_call | solution.py:84
  2.2 2.1 %collective-permute-start.2 = (bf16[2,144,256]{2,1,0:T(8,128)(2,1)S(1)}, bf16[2,144,256]{2,1,0:T(8,128)(2,1)S(1)}, u32[]{:S(2)}, u32[]{:S(2)}) collective-permute-start(bf16[2,144,256]{2,1,0:T(8,128)(2,1)S(1)} %get-tuple-element.15.refs_1_), channel_id=1, source_target_pairs={{0,1},{1,0},{2,3},{3,2},{4,5},{5,4},{6,7},{7,6},{8,9},{9,8},{10,11... | collective-permute-start | bytes 442376 | tf_op jit(solution)/shard_map/ppermute | solution.py:294
  4.3 0.7 %collective-permute-start.1 = (bf16[2,144,256]{2,1,0:T(8,128)(2,1)S(1)}, bf16[2,144,256]{2,1,0:T(8,128)(2,1)S(1)}, u32[]{:S(2)}, u32[]{:S(2)}) collective-permute-start(bf16[2,144,256]{2,1,0:T(8,128)(2,1)S(1)} %get-tuple-element.15.refs_1_), channel_id=1, source_target_pairs={{8,16},{16,8},{9,17},{17,9},{10,18},{18,10},{11,19},{19,11},{12,20... | collective-permute-start | bytes 442376 | tf_op jit(solution)/shard_map/ppermute | solution.py:294
  5.0 3.9 %collective-permute-start = (bf16[2,144,256]{2,1,0:T(8,128)(2,1)S(1)}, bf16[2,144,256]{2,1,0:T(8,128)(2,1)S(1)}, u32[]{:S(2)}, u32[]{:S(2)}) collective-permute-start(bf16[2,144,256]{2,1,0:T(8,128)(2,1)S(1)} %get-tuple-element.15.refs_1_), channel_id=1, source_target_pairs={{0,8},{8,0},{16,24},{24,16},{1,9},{9,1},{17,25},{25,17},{2,10},{10... | collective-permute-start | bytes 442376 | tf_op jit(solution)/shard_map/ppermute | solution.py:294
  8.9 1.5 %collective-permute-start.3 = (bf16[144,256]{1,0:T(8,128)(2,1)S(1)}, bf16[144,256]{1,0:T(8,128)(2,1)S(1)}, u32[]{:S(2)}, u32[]{:S(2)}) collective-permute-start(bf16[144,256]{1,0:T(8,128)(2,1)S(1)} %get-tuple-element.16), channel_id=1, source_target_pairs={{0,2},{2,0},{4,6},{6,4},{1,3},{3,1},{5,7},{7,5},{8,10},{10,8},{12,... | collective-permute-start | bytes 221192 | tf_op jit(solution)/shard_map/ppermute | solution.py:310
  10.4 3.0 %collective-permute-start.4 = (bf16[144,256]{1,0:T(8,128)(2,1)S(1)}, bf16[144,256]{1,0:T(8,128)(2,1)S(1)}, u32[]{:S(2)}, u32[]{:S(2)}) collective-permute-start(bf16[144,256]{1,0:T(8,128)(2,1)S(1)} %get-tuple-element.17), channel_id=1, source_target_pairs={{2,4},{4,2},{3,5},{5,3},{10,12},{12,10},{11,13},{13,11},{18,20},{2... | collective-permute-start | bytes 221192 | tf_op jit(solution)/shard_map/ppermute | solution.py:310
  13.4 0.0 collective-permute-done.3.refs_5_
  13.4 2.6 %collective-permute-done.4.refs_6_ = bf16[144,256]{1,0:T(8,128)(2,1)S(1)} collective-permute-done((bf16[144,256]{1,0:T(8,128)(2,1)S(1)}, bf16[144,256]{1,0:T(8,128)(2,1)S(1)}, u32[]{:S(2)}, u32[]{:S(2)}) %collective-permute-start.4) | collective-permute-done | bytes 73760 | tf_op jit(solution)/shard_map/ppermute | solution.py:310
  16.1 0.0 collective-permute-done.2.refs_4_
  16.1 0.0 collective-permute-done.1.refs_3_
  16.1 0.0 collective-permute-done.refs_2_
  16.1 0.0 copy-start.11
  16.1 0.0 copy-start.10
  16.1 0.0 copy-start.13
  16.1 0.0 copy-done.5
  16.1 0.0 copy-done.6
  16.1 0.6 %copy-done.11 = f32[256]{0:T(256)S(1)} copy-done((f32[256]{0:T(256)S(1)}, f32[256]{0:T(256)}, u32[]{:S(2)}) %copy-start.11) | copy-done | bytes 1048
  16.8 0.0 copy-done.10
  16.8 0.0 copy-done.13
  16.8 0.0 copy-start
  16.8 1.0 %copy-done = bf16[256,1024]{1,0:T(8,128)(2,1)S(1)} copy-done((bf16[256,1024]{1,0:T(8,128)(2,1)S(1)}, bf16[256,1024]{1,0:T(8,128)(2,1)}, u32[]{:S(2)}) %copy-start) | copy-done | bytes 524312
  17.8 0.0 copy-start.2
  17.8 1.0 %copy-done.2 = bf16[1024,256]{1,0:T(8,128)(2,1)S(1)} copy-done((bf16[1024,256]{1,0:T(8,128)(2,1)S(1)}, bf16[1024,256]{1,0:T(8,128)(2,1)}, u32[]{:S(2)}) %copy-start.2) | copy-done | bytes 524312
  18.9 0.0 copy-start.7
  18.9 0.9 %copy-done.7 = bf16[256,256]{1,0:T(8,128)(2,1)S(1)} copy-done((bf16[256,256]{1,0:T(8,128)(2,1)S(1)}, bf16[256,256]{1,0:T(8,128)(2,1)}, u32[]{:S(2)}) %copy-start.7) | copy-done | bytes 131096
  19.8 0.0 copy-start.9
  19.8 0.9 %copy-done.9 = bf16[256,256]{1,0:T(8,128)(2,1)S(1)} copy-done((bf16[256,256]{1,0:T(8,128)(2,1)S(1)}, bf16[256,256]{1,0:T(8,128)(2,1)}, u32[]{:S(2)}) %copy-start.9) | copy-done | bytes 131096
  20.7 0.0 copy-start.1
  20.7 0.0 copy-start.3
  20.7 9.6 %layer_features_travel.1 = (bf16[2,144,256]{2,1,0:T(8,128)(2,1)S(1)}, f32[128,256]{1,0:T(8,128)S(1)}) custom-call(f32[2,128,256]{2,1,0:T(8,128)S(1)} %bitcast.9, bf16[2,144,256]{2,1,0:T(8,128)(2,1)S(1)} %get-tuple-element.15.refs_1_, bf16[2,144,256]{2,1,0:T(8,128)(2,1)S(1)} %collective-permute-done.refs_2_, ...), custom_call_target="tpu_custom_call" | custom-call | tf_op jit(solution)/shard_map/layer_features_travel/pallas_call | solution.py:233
  30.3 0.3 collective-permute-start.5
  30.6 3.8 %collective-permute-done.5.arrived = bf16[2,144,256]{2,1,0:T(8,128)(2,1)S(1)} collective-permute-done((bf16[2,144,256]{2,1,0:T(8,128)(2,1)S(1)}, bf16[2,144,256]{2,1,0:T(8,128)(2,1)S(1)}, u32[]{:S(2)}, u32[]{:S(2)}) %collective-permute-start.5) | collective-permute-done | bytes 147488 | tf_op jit(solution)/shard_map/ppermute | solution.py:320
  34.3 0.0 copy-start.8
  34.3 0.1 settle.1
  34.4 0.7 %collective-permute-start.7 = (bf16[2,144,256]{2,1,0:T(8,128)(2,1)S(1)}, bf16[2,144,256]{2,1,0:T(8,128)(2,1)S(1)}, u32[]{:S(2)}, u32[]{:S(2)}) collective-permute-start(bf16[2,144,256]{2,1,0:T(8,128)(2,1)S(1)} %get-tuple-element.21.refs_1_), channel_id=1, source_target_pairs={{8,16},{16,8},{9,17},{17,9},{10,18},{18,10},{11,19},{19,11},{12,20... | collective-permute-start | bytes 442376 | tf_op jit(solution)/shard_map/ppermute | solution.py:294
  35.1 2.8 %collective-permute-start.6 = (bf16[2,144,256]{2,1,0:T(8,128)(2,1)S(1)}, bf16[2,144,256]{2,1,0:T(8,128)(2,1)S(1)}, u32[]{:S(2)}, u32[]{:S(2)}) collective-permute-start(bf16[2,144,256]{2,1,0:T(8,128)(2,1)S(1)} %get-tuple-element.21.refs_1_), channel_id=1, source_target_pairs={{0,8},{8,0},{16,24},{24,16},{1,9},{9,1},{17,25},{25,17},{2,10},{10... | collective-permute-start | bytes 442376 | tf_op jit(solution)/shard_map/ppermute | solution.py:294
  38.0 1.0 %collective-permute-start.8 = (bf16[144,256]{1,0:T(8,128)(2,1)S(1)}, bf16[144,256]{1,0:T(8,128)(2,1)S(1)}, u32[]{:S(2)}, u32[]{:S(2)}) collective-permute-start(bf16[144,256]{1,0:T(8,128)(2,1)S(1)} %get-tuple-element.23), channel_id=1, source_target_pairs={{0,2},{2,0},{4,6},{6,4},{1,3},{3,1},{5,7},{7,5},{8,10},{10,8},{12,... | collective-permute-start | bytes 221192 | tf_op jit(solution)/shard_map/ppermute | solution.py:310
  38.9 2.4 %collective-permute-start.9 = (bf16[144,256]{1,0:T(8,128)(2,1)S(1)}, bf16[144,256]{1,0:T(8,128)(2,1)S(1)}, u32[]{:S(2)}, u32[]{:S(2)}) collective-permute-start(bf16[144,256]{1,0:T(8,128)(2,1)S(1)} %get-tuple-element.24), channel_id=1, source_target_pairs={{2,4},{4,2},{3,5},{5,3},{10,12},{12,10},{11,13},{13,11},{18,20},{2... | collective-permute-start | bytes 221192 | tf_op jit(solution)/shard_map/ppermute | solution.py:310
  41.3 0.0 collective-permute-done.8.refs_5_
  41.3 3.3 %collective-permute-done.9.refs_6_ = bf16[144,256]{1,0:T(8,128)(2,1)S(1)} collective-permute-done((bf16[144,256]{1,0:T(8,128)(2,1)S(1)}, bf16[144,256]{1,0:T(8,128)(2,1)S(1)}, u32[]{:S(2)}, u32[]{:S(2)}) %collective-permute-start.9) | collective-permute-done | bytes 73760 | tf_op jit(solution)/shard_map/ppermute | solution.py:310
  44.6 0.0 collective-permute-done.7.refs_3_
  44.6 0.0 collective-permute-done.6.refs_2_
  44.6 0.0 copy-done.1
  44.6 0.0 copy-done.3
  44.6 0.0 copy-done.8
  44.6 9.8 %layer_settled_bins.1 = f32[2,128,256]{2,1,0:T(8,128)} custom-call(f32[2,128,256]{2,1,0:T(8,128)S(1)} %get-tuple-element.20.refs_0_, bf16[2,144,256]{2,1,0:T(8,128)(2,1)S(1)} %get-tuple-element.21.refs_1_, bf16[2,144,256]{2,1,0:T(8,128)(2,1)S(1)} %collective-permute-done.6.refs_2_, bf16[2,144,256]{2,1,0:T(8,128)(2,1)S(1)} %collective-permute-done.7.refs_3_, ...), custom_call_target="tpu_custom_call" | custom-call | tf_op jit(solution)/shard_map/layer_settled_bins/pallas_call | solution.py:233
Async XLA Ops:
  0.0 0.7 %copy-start.12 = (s32[1,2,1]{1,2,0:T(1,128)S(1)}, s32[1,2,1]{1,2,0:T(1,128)}, u32[]{:S(2)}) copy-start(s32[1,2,1]{1,2,0:T(1,128)} %param.12) | copy-start | bytes 28
  0.7 0.9 %copy-start.4 = (f32[1,2,1,128,256]{4,3,2,1,0:T(8,128)S(1)}, f32[1,2,1,128,256]{4,3,2,1,0:T(8,128)}, u32[]{:S(2)}) copy-start(f32[1,2,1,128,256]{4,3,2,1,0:T(8,128)} %param.11) | copy-start | bytes 786436
  1.6 14.5 %copy-start.5 = (bf16[256,256]{1,0:T(8,128)(2,1)S(1)}, bf16[256,256]{1,0:T(8,128)(2,1)}, u32[]{:S(2)}) copy-start(bf16[256,256]{1,0:T(8,128)(2,1)} %refs_7_.3) | copy-start | bytes 393220
  1.6 14.5 %copy-start.6 = (bf16[256,256]{1,0:T(8,128)(2,1)S(1)}, bf16[256,256]{1,0:T(8,128)(2,1)}, u32[]{:S(2)}) copy-start(bf16[256,256]{1,0:T(8,128)(2,1)} %refs_8_.3) | copy-start | bytes 393220
  2.2 13.9 %collective-permute-start.2 = (bf16[2,144,256]{2,1,0:T(8,128)(2,1)S(1)}, bf16[2,144,256]{2,1,0:T(8,128)(2,1)S(1)}, u32[]{:S(2)}, u32[]{:S(2)}) collective-permute-start(bf16[2,144,256]{2,1,0:T(8,128)(2,1)S(1)} %get-tuple-element.15.refs_1_), channel_id=1, source_target_pairs={{0,1},{1,0},{2,3},{3,2},{4,5},{5,4},{6,7},{7,6},{8,9},{9,8},{10,11... | collective-permute-start | bytes 442376 | tf_op jit(solution)/shard_map/ppermute | solution.py:294
  4.3 11.7 %collective-permute-start.1 = (bf16[2,144,256]{2,1,0:T(8,128)(2,1)S(1)}, bf16[2,144,256]{2,1,0:T(8,128)(2,1)S(1)}, u32[]{:S(2)}, u32[]{:S(2)}) collective-permute-start(bf16[2,144,256]{2,1,0:T(8,128)(2,1)S(1)} %get-tuple-element.15.refs_1_), channel_id=1, source_target_pairs={{8,16},{16,8},{9,17},{17,9},{10,18},{18,10},{11,19},{19,11},{12,20... | collective-permute-start | bytes 442376 | tf_op jit(solution)/shard_map/ppermute | solution.py:294
  5.0 11.1 %collective-permute-start = (bf16[2,144,256]{2,1,0:T(8,128)(2,1)S(1)}, bf16[2,144,256]{2,1,0:T(8,128)(2,1)S(1)}, u32[]{:S(2)}, u32[]{:S(2)}) collective-permute-start(bf16[2,144,256]{2,1,0:T(8,128)(2,1)S(1)} %get-tuple-element.15.refs_1_), channel_id=1, source_target_pairs={{0,8},{8,0},{16,24},{24,16},{1,9},{9,1},{17,25},{25,17},{2,10},{10... | collective-permute-start | bytes 442376 | tf_op jit(solution)/shard_map/ppermute | solution.py:294
  8.9 4.5 %collective-permute-start.3 = (bf16[144,256]{1,0:T(8,128)(2,1)S(1)}, bf16[144,256]{1,0:T(8,128)(2,1)S(1)}, u32[]{:S(2)}, u32[]{:S(2)}) collective-permute-start(bf16[144,256]{1,0:T(8,128)(2,1)S(1)} %get-tuple-element.16), channel_id=1, source_target_pairs={{0,2},{2,0},{4,6},{6,4},{1,3},{3,1},{5,7},{7,5},{8,10},{10,8},{12,... | collective-permute-start | bytes 221192 | tf_op jit(solution)/shard_map/ppermute | solution.py:310
  10.4 5.7 %collective-permute-start.4 = (bf16[144,256]{1,0:T(8,128)(2,1)S(1)}, bf16[144,256]{1,0:T(8,128)(2,1)S(1)}, u32[]{:S(2)}, u32[]{:S(2)}) collective-permute-start(bf16[144,256]{1,0:T(8,128)(2,1)S(1)} %get-tuple-element.17), channel_id=1, source_target_pairs={{2,4},{4,2},{3,5},{5,3},{10,12},{12,10},{11,13},{13,11},{18,20},{2... | collective-permute-start | bytes 221192 | tf_op jit(solution)/shard_map/ppermute | solution.py:310
  16.1 0.7 %copy-start.11 = (f32[256]{0:T(256)S(1)}, f32[256]{0:T(256)}, u32[]{:S(2)}) copy-start(f32[256]{0:T(256)} %param.21) | copy-start | bytes 3076
  16.1 0.7 %copy-start.10 = (f32[256]{0:T(256)S(1)}, f32[256]{0:T(256)}, u32[]{:S(2)}) copy-start(f32[256]{0:T(256)} %param.20) | copy-start | bytes 3076
  16.1 0.7 %copy-start.13 = (s32[1,2,1]{1,2,0:T(1,128)S(1)}, s32[1,2,1]{1,2,0:T(1,128)}, u32[]{:S(2)}) copy-start(s32[1,2,1]{1,2,0:T(1,128)} %param.13) | copy-start | bytes 28
  16.8 1.0 %copy-start = (bf16[256,1024]{1,0:T(8,128)(2,1)S(1)}, bf16[256,1024]{1,0:T(8,128)(2,1)}, u32[]{:S(2)}) copy-start(bf16[256,1024]{1,0:T(8,128)(2,1)} %refs_11_.3) | copy-start | bytes 1572868
  17.8 1.0 %copy-start.2 = (bf16[1024,256]{1,0:T(8,128)(2,1)S(1)}, bf16[1024,256]{1,0:T(8,128)(2,1)}, u32[]{:S(2)}) copy-start(bf16[1024,256]{1,0:T(8,128)(2,1)} %refs_12_.3) | copy-start | bytes 1572868
  18.9 0.9 %copy-start.7 = (bf16[256,256]{1,0:T(8,128)(2,1)S(1)}, bf16[256,256]{1,0:T(8,128)(2,1)}, u32[]{:S(2)}) copy-start(bf16[256,256]{1,0:T(8,128)(2,1)} %refs_9_.3) | copy-start | bytes 393220
  19.8 0.9 %copy-start.9 = (bf16[256,256]{1,0:T(8,128)(2,1)S(1)}, bf16[256,256]{1,0:T(8,128)(2,1)}, u32[]{:S(2)}) copy-start(bf16[256,256]{1,0:T(8,128)(2,1)} %refs_10_.3) | copy-start | bytes 393220
  20.7 23.9 %copy-start.1 = (bf16[256,1024]{1,0:T(8,128)(2,1)S(1)}, bf16[256,1024]{1,0:T(8,128)(2,1)}, u32[]{:S(2)}) copy-start(bf16[256,1024]{1,0:T(8,128)(2,1)} %refs_11_.3) | copy-start | bytes 1572868
  20.7 23.9 %copy-start.3 = (bf16[1024,256]{1,0:T(8,128)(2,1)S(1)}, bf16[1024,256]{1,0:T(8,128)(2,1)}, u32[]{:S(2)}) copy-start(bf16[1024,256]{1,0:T(8,128)(2,1)} %refs_12_.3) | copy-start | bytes 1572868
  30.3 4.1 %collective-permute-start.5 = (bf16[2,144,256]{2,1,0:T(8,128)(2,1)S(1)}, bf16[2,144,256]{2,1,0:T(8,128)(2,1)S(1)}, u32[]{:S(2)}, u32[]{:S(2)}) collective-permute-start(bf16[2,144,256]{2,1,0:T(8,128)(2,1)S(1)} %get-tuple-element.18.travel), channel_id=1, source_target_pairs={{0,1},{1,0},{2,3},{3,2},{4,5},{5,4},{6,7},{7,6},{8,9},{9,8},{10,11... | collective-permute-start | bytes 442376 | tf_op jit(solution)/shard_map/ppermute | solution.py:320
  34.3 10.3 %copy-start.8 = (bf16[256,256]{1,0:T(8,128)(2,1)S(1)}, bf16[256,256]{1,0:T(8,128)(2,1)}, u32[]{:S(2)}) copy-start(bf16[256,256]{1,0:T(8,128)(2,1)} %refs_9_.3) | copy-start | bytes 393220
  34.4 10.1 %collective-permute-start.7 = (bf16[2,144,256]{2,1,0:T(8,128)(2,1)S(1)}, bf16[2,144,256]{2,1,0:T(8,128)(2,1)S(1)}, u32[]{:S(2)}, u32[]{:S(2)}) collective-permute-start(bf16[2,144,256]{2,1,0:T(8,128)(2,1)S(1)} %get-tuple-element.21.refs_1_), channel_id=1, source_target_pairs={{8,16},{16,8},{9,17},{17,9},{10,18},{18,10},{11,19},{19,11},{12,20... | collective-permute-start | bytes 442376 | tf_op jit(solution)/shard_map/ppermute | solution.py:294
  35.1 9.5 %collective-permute-start.6 = (bf16[2,144,256]{2,1,0:T(8,128)(2,1)S(1)}, bf16[2,144,256]{2,1,0:T(8,128)(2,1)S(1)}, u32[]{:S(2)}, u32[]{:S(2)}) collective-permute-start(bf16[2,144,256]{2,1,0:T(8,128)(2,1)S(1)} %get-tuple-element.21.refs_1_), channel_id=1, source_target_pairs={{0,8},{8,0},{16,24},{24,16},{1,9},{9,1},{17,25},{25,17},{2,10},{10... | collective-permute-start | bytes 442376 | tf_op jit(solution)/shard_map/ppermute | solution.py:294
  38.0 3.3 %collective-permute-start.8 = (bf16[144,256]{1,0:T(8,128)(2,1)S(1)}, bf16[144,256]{1,0:T(8,128)(2,1)S(1)}, u32[]{:S(2)}, u32[]{:S(2)}) collective-permute-start(bf16[144,256]{1,0:T(8,128)(2,1)S(1)} %get-tuple-element.23), channel_id=1, source_target_pairs={{0,2},{2,0},{4,6},{6,4},{1,3},{3,1},{5,7},{7,5},{8,10},{10,8},{12,... | collective-permute-start | bytes 221192 | tf_op jit(solution)/shard_map/ppermute | solution.py:310
  38.9 5.7 %collective-permute-start.9 = (bf16[144,256]{1,0:T(8,128)(2,1)S(1)}, bf16[144,256]{1,0:T(8,128)(2,1)S(1)}, u32[]{:S(2)}, u32[]{:S(2)}) collective-permute-start(bf16[144,256]{1,0:T(8,128)(2,1)S(1)} %get-tuple-element.24), channel_id=1, source_target_pairs={{2,4},{4,2},{3,5},{5,3},{10,12},{12,10},{11,13},{13,11},{18,20},{2... | collective-permute-start | bytes 221192 | tf_op jit(solution)/shard_map/ppermute | solution.py:310

commit v2 on v1

v2 whole, which is shorter than its diff:
```python
import jax
import jax.numpy as jnp
from jax import lax
from jax.experimental import pallas as pl
from jax.experimental.pallas import tpu as pltpu
from jax.sharding import PartitionSpec as P

HEADS = 8
EPSILON = 1e-05
LOG2E = 1.4426950408889634
DEAD = -1e30
HEAD_ROWS = 16
ROLES = 2

F32 = jnp.float32
BF16 = jnp.bfloat16

VMEM = pl.BlockSpec(memory_space=pltpu.VMEM)
SMEM = pl.BlockSpec(memory_space=pltpu.SMEM)
ROWS = (((1,), (1,)), ((), ()))
COLUMNS = (((0,), (1,)), ((), ()))
TURNED = (((0,), (0,)), ((), ()))


def shape(dims, dtype):
    return jax.ShapeDtypeStruct(dims, dtype)


def call(body, outs, specs, scratch=(), limit=30 << 20):
    return pl.pallas_call(
        body,
        out_shape=outs,
        in_specs=specs,
        out_specs=jax.tree.map(lambda _: VMEM, outs),
        scratch_shapes=scratch,
        compiler_params=pltpu.CompilerParams(vmem_limit_bytes=limit),
    )


def swaps(count, parity, around=False):
    pairs = []
    for low in range(parity, count - 1, 2):
        pairs += [(low, low + 1), (low + 1, low)]
    if around and parity == 1 and count % 2 == 0 and count > 2:
        pairs += [(0, count - 1), (count - 1, 0)]
    return pairs


def dot(a, b, dims=(((1,), (0,)), ((), ()))):
    return lax.dot_general(a, b, dims, preferred_element_type=F32)


def layer_norm(values, gain):
    centre = values - jnp.mean(values, axis=-1, keepdims=True)
    spread = jnp.mean(centre * centre, axis=-1, keepdims=True)
    return centre * lax.rsqrt(spread + EPSILON) * gain


def live_rows(block, slots, present=None):
    count = block[slots : slots + 1, :128].astype(F32)
    if present is not None:
        count = jnp.where(present, count, 0.0)
    row = lax.broadcasted_iota(jnp.int32, (slots, 128), 0).astype(F32)
    return jnp.where(row < count, 0.0, DEAD).astype(BF16)


def prepare_body(out):
    out[...] = jnp.zeros_like(out)


def prepare(slots, width):
    return pl.pallas_call(
        prepare_body,
        out_shape=shape((8, 128), F32),
        out_specs=VMEM,
        compiler_params=pltpu.CompilerParams(vmem_limit_bytes=1 << 20),
        cost_estimate=pl.CostEstimate(
            flops=80000 * slots * width, transcendentals=0, bytes_accessed=0
        ),
        name="prepare",
    )()


def pack_body(features, counts, ready, both, first, second, residual):
    slots, width = features.shape[1:]
    parity = lax.axis_index("gy") % 2
    del ready
    for role, single in ((0, first), (1, second)):
        held = 1 - parity if role == 0 else parity
        state = features[held]
        residual[role] = state
        rows = state.astype(BF16)
        row = lax.broadcasted_iota(jnp.int32, (HEAD_ROWS, width), 0)
        top = jnp.where(row == 1, role, counts[held]).astype(F32).astype(BF16)
        both[role, :slots] = rows
        both[role, slots:] = top
        single[:slots] = rows
        single[slots:] = top


def pack(features, counts, ready):
    bins, slots, width = features.shape
    tall = slots + HEAD_ROWS
    outs = [
        shape((bins, tall, width), BF16),
        shape((tall, width), BF16),
        shape((tall, width), BF16),
        shape((bins, slots, width), F32),
    ]
    return call(pack_body, outs, [VMEM, SMEM, VMEM])(features, counts, ready)


def score_keys(keys, biases, width):
    bias = jnp.concatenate(biases, axis=0)
    return [
        jnp.concatenate([keys[:, at : at + 128], bias], axis=1) for at in range(0, width, 128)
    ]


def pick(array, places, slots, axis):
    parts = [lax.slice_in_dim(array, p * slots, (p + 1) * slots, axis=axis) for p in places]
    return jnp.concatenate(parts, axis=axis)


def early(own, near, query_weight, key_weight, value_weight, outs):
    turned_values, masks, powers, peaks, sums = outs
    width = own.shape[-1]
    slots = own.shape[1] - HEAD_ROWS
    head_size = width // HEADS
    per_group = HEADS * 128 // width
    factor = head_size ** (-0.5) * LOG2E
    blocks = [own[0], own[1]] + [h[role] for role in range(ROLES) for h in near]
    rows = jnp.concatenate([b[:slots] for b in blocks], axis=0)
    biases = [live_rows(b, slots) for b in blocks]
    queries = dot(rows[: ROLES * slots], query_weight[...]).astype(BF16)
    keys = dot(rows, key_weight[...]).astype(BF16)
    lane = lax.broadcasted_iota(jnp.int32, (slots, 128), 1)
    mark = jnp.where(lane == 0, 1.0, 0.0).astype(BF16)
    places = [
        [0, 1] + [2 + role * len(near) + n for n in range(len(near))] for role in range(ROLES)
    ]
    for role in range(ROLES):
        part = score_keys(
            pick(keys, places[role], slots, 0), [biases[p] for p in places[role]], width
        )
        for pair in range(HEADS // 2):
            masked = []
            for head in (2 * pair, 2 * pair + 1):
                group, inner = divmod(head, per_group)
                query = queries[role * slots : (role + 1) * slots]
                query = query[:, group * 128 : (group + 1) * 128]
                inside = (lane >= inner * head_size) & (lane < (inner + 1) * head_size)
                query = jnp.where(inside, query.astype(F32), 0.0).astype(BF16)
                masked.append(jnp.concatenate([query, mark], axis=1))
            masked = jnp.concatenate(masked, axis=0)
            at = role * (HEADS // 2) + pair
            masks[at] = masked
            scores = dot(part[2 * pair // per_group], masked, ROWS)
            peak = jnp.max(scores, axis=0, keepdims=True)
            power = jnp.exp2((scores - peak) * factor)
            powers[at] = power
            peaks[at] = peak
            sums[at] = jnp.sum(power, axis=0, keepdims=True)
    values = dot(value_weight[...], rows, COLUMNS).astype(BF16)
    for role in range(ROLES):
        turned_values[role] = pick(values, places[role], slots, 1)


def early_shapes(slots, width, near):
    keys = (2 + near) * slots
    pairs = ROLES * HEADS // 2
    return [
        shape((ROLES, width, keys), BF16),
        shape((pairs, 2 * slots, 256), BF16),
        shape((pairs, keys, 2 * slots), F32),
        shape((pairs, 1, 2 * slots), F32),
        shape((pairs, 1, 2 * slots), F32),
    ]


def run_early(own, near, weights):
    slots, width = own.shape[1] - HEAD_ROWS, own.shape[2]

    def body(own, *refs):
        n = len(near)
        early(own, refs[:n], *refs[n : n + 3], refs[n + 3 :])

    outs = early_shapes(slots, width, len(near))
    return call(body, outs, [VMEM] * (4 + len(near)))(own, *near, *weights[:3])


def late(residual, own, far, sides, flags, prior, weights, gains):
    turned_own, masks, powers, peaks, sums = prior
    _, key_weight, value_weight, out_weight, up_weight, down_weight = weights
    attention_gain, feed_gain = gains
    slots, width = residual.shape[1:]
    head_size = width // HEADS
    per_group = HEADS * 128 // width
    factor = head_size ** (-0.5) * LOG2E
    blocks, biases = [], []
    for role in range(ROLES):
        near = [(h[role], flag) for h, flag in far] + [(sides[role][...], flags[role])]
        for block, flag in near:
            blocks.append(block[:slots])
            biases.append(live_rows(block, slots, flag))
    count = len(blocks) // ROLES
    rows = jnp.concatenate(blocks, axis=0)
    keys = dot(rows, key_weight[...]).astype(BF16)
    values = dot(value_weight[...], rows, COLUMNS).astype(BF16)
    attended = []
    for role in range(ROLES):
        span = slice(role * count * slots, (role + 1) * count * slots)
        part = score_keys(keys[span], biases[role * count : (role + 1) * count], width)
        pieces = []
        for pair in range(HEADS // 2):
            at = role * (HEADS // 2) + pair
            scores = dot(part[2 * pair // per_group], masks[at], ROWS)
            before = peaks[at]
            peak = jnp.maximum(jnp.max(scores, axis=0, keepdims=True), before)
            power = jnp.exp2((scores - peak) * factor)
            rescale = jnp.exp2((before - peak) * factor)
            total = jnp.sum(power, axis=0, keepdims=True) + sums[at] * rescale
            inverse = 1.0 / total
            feature = slice(2 * pair * head_size, 2 * (pair + 1) * head_size)
            mixed = dot(values[feature, span], (power * inverse).astype(BF16)) + dot(
                turned_own[role, feature], (powers[at] * (rescale * inverse)).astype(BF16)
            )
            pieces += [mixed[:head_size, :slots], mixed[head_size:, slots:]]
        attended.append(jnp.concatenate(pieces, axis=0).astype(BF16))
    mixed = jnp.concatenate([dot(a, out_weight[...], TURNED) for a in attended], axis=0)
    state = jnp.concatenate([residual[0], residual[1]], axis=0)
    hidden = layer_norm(state + mixed, attention_gain[...])
    inner = jax.nn.gelu(dot(hidden.astype(BF16), up_weight[...])).astype(BF16)
    result = layer_norm(hidden + dot(inner, down_weight[...]), feed_gain[...])
    row = lax.broadcasted_iota(jnp.int32, (slots, width), 0).astype(F32)
    results = []
    for role in range(ROLES):
        live = row < own[role, slots : slots + 1, :].astype(F32)
        results.append(jnp.where(live, result[role * slots : (role + 1) * slots], 0.0))
    return results


def travel_body(results, own, places, spans, travel, stayed):
    slots, width = stayed.shape
    parity = lax.axis_index("gy") % 2
    span_z = spans[1]
    line = lax.broadcasted_iota(jnp.int32, (HEAD_ROWS, width), 0)
    for role in range(ROLES):
        place = places[1 - parity if role == 0 else parity]
        stays = place % span_z == lax.axis_index("gz")
        new_role = jnp.where((place // span_z) % 2 == parity, 1, 0)
        slot = jnp.where(stays, 1, 0)
        travel[slot, :slots] = results[role].astype(BF16)
        top = own[role, slots:].astype(F32)
        travel[slot, slots:] = jnp.where(line == 1, new_role.astype(F32), top).astype(BF16)

        @pl.when(stays)
        def _():
            stayed[...] = results[role]


def run_late(end, spans, residual, own, far, sides, around, prior, weights, gains, places=None):
    bins, slots, width = residual.shape
    tall = slots + HEAD_ROWS
    halos = [block for block, _ in far]
    args = [residual, own, *halos, *sides, *prior, *weights, *gains]
    specs = [VMEM] * len(args)
    if end == "bins":
        outs = [shape((bins, slots, width), F32)]
    else:
        outs = [shape((bins, tall, width), BF16), shape((slots, width), F32)]
        args.append(places)
        specs.append(SMEM)

    def inside(axis):
        if not around:
            return None
        index = lax.axis_index(axis)
        return (index > 0) & (index < lax.axis_size(axis) - 1)

    def body(*refs):
        ins, results = list(refs[: len(args)]), refs[len(args) :]

        def take(count):
            taken = ins[:count]
            del ins[:count]
            return taken

        residual, own = take(2)
        blocks = take(len(halos))
        flagged = [
            (block, inside(axis) if axis else None) for block, (_, axis) in zip(blocks, far)
        ]
        side_refs = take(2)
        flags = (None, inside("gy"))
        prior_refs, weight_refs, gain_refs = take(5), take(6), take(2)
        rows = late(
            residual, own, flagged, side_refs, flags, prior_refs, weight_refs, gain_refs
        )
        if end == "bins":
            (out,) = results
            parity = lax.axis_index("gy") % 2
            out[1 - parity] = rows[0]
            out[parity] = rows[1]
        else:
            travel_body(rows, own, ins[0], spans, *results)

    return call(body, outs, specs)(*args)


def choose(role, yes, no):
    return jnp.where(role < 0.5, yes.astype(F32), no.astype(F32))


def settle_body(travel, arrived, stayed, both, first, second, beside, residual):
    slots = stayed.shape[0]
    stay, came = travel[1], arrived[0]
    role = stay[slots + 1 : slots + 2].astype(F32)
    for index, single in ((0, first), (1, second)):
        block = choose(role, *((stay, came) if index == 0 else (came, stay))).astype(BF16)
        both[index] = block
        single[...] = block
        rows = stayed[...], came[:slots]
        residual[index] = choose(role, *(rows if index == 0 else rows[::-1]))
    peer, left = arrived[1], travel[0]
    role = peer[slots + 1 : slots + 2].astype(F32)
    beside[0] = choose(role, peer, left).astype(BF16)
    beside[1] = choose(role, left, peer).astype(BF16)


def settle(travel, arrived, stayed):
    bins, tall, width = travel.shape
    slots = stayed.shape[0]
    outs = [
        shape((bins, tall, width), BF16),
        shape((tall, width), BF16),
        shape((tall, width), BF16),
        shape((bins, tall, width), BF16),
        shape((bins, slots, width), F32),
    ]
    return call(settle_body, outs, [VMEM] * 3)(travel, arrived, stayed)


def relocate(state, counts, dest_bin, bins_y):
    total, slots, width = state.shape
    depth = lax.axis_size("gz")
    targets = dest_bin.reshape(-1)
    peer = targets % depth
    local = targets // depth % bins_y
    order = jnp.arange(total, dtype=jnp.int32)
    earlier = (peer[None, :] == peer[:, None]) & (order[None, :] < order[:, None])
    slot = jnp.sum(earlier.astype(jnp.int32), axis=1)
    capacity = (total + depth - 1) // depth
    outgoing = jnp.zeros((depth, capacity, slots, width), F32).at[peer, slot].set(state)
    outgoing_counts = jnp.zeros((depth, capacity), jnp.int32).at[peer, slot].set(counts)
    outgoing_places = jnp.full((depth, capacity), total, jnp.int32).at[peer, slot].set(local)
    arrived = lax.all_to_all(outgoing.astype(BF16), "gz", 0, 0, tiled=True).astype(F32)
    arrived_counts = lax.all_to_all(outgoing_counts, "gz", 0, 0, tiled=True)
    places = lax.all_to_all(outgoing_places, "gz", 0, 0, tiled=True).reshape(-1)
    moved = jnp.zeros((total, slots, width), F32)
    moved = moved.at[places].set(arrived.reshape(-1, slots, width), mode="drop")
    moved_counts = jnp.zeros((total,), jnp.int32)
    moved_counts = moved_counts.at[places].set(arrived_counts.reshape(-1), mode="drop")
    return moved, moved_counts


def exchange(own, first, second, axes, around):
    far = []
    for axis in axes:
        count = lax.axis_size(axis)
        for parity in range(2):
            pairs = swaps(count, parity, around)
            if not pairs:
                continue
            block = lax.ppermute(own, axis, pairs)
            far.append((block, axis if around and parity == 1 else None))
    sides = []
    for parity, block in ((0, first), (1, second)):
        sides.append(
            lax.ppermute(block, "gy", swaps(lax.axis_size("gy"), parity, around))
        )
    return far, sides


def shards(features, occupancy, dest_bin, *rest):
    weights, gains = rest[:6], [g.reshape(1, -1) for g in rest[6:]]
    slots, width = features.shape[3:]
    state = features.reshape(2, slots, width)
    counts = occupancy.reshape(2)
    places = dest_bin.reshape(2)
    depth = lax.axis_size("gz")
    spans = (2 * lax.axis_size("gy"), depth)

    ready = prepare(slots, width)
    own, first, second, residual = pack(state, counts, ready)
    far, sides = exchange(own, first, second, ("gx", "gz"), True)
    prior = run_early(own, [], weights)
    end = "travel" if depth == 2 else "bins"
    results = run_late(
        end, spans, residual, own, far, sides, True, prior, weights, gains,
        places if depth == 2 else None,
    )
    if depth == 2:
        travel, stayed = results
        arrived = lax.ppermute(travel, "gz", swaps(depth, 0))
        own, first, second, beside, residual = settle(travel, arrived, stayed)
        near, axes = [beside], ("gx",)
    else:
        state, counts = relocate(results[0], counts, places, 2)
        own, first, second, residual = pack(state, counts, ready)
        near, axes = [], ("gx", "gz")
    far, sides = exchange(own, first, second, axes, False)
    prior = run_early(own, near, weights)
    (out,) = run_late(
        "bins", spans, residual, own, far, sides, False, prior, weights, gains
    )
    return out.reshape(features.shape)


def solution(mesh):
    placed = (
        P("gx", "gy", "gz", None, None),
        P("gx", "gy", "gz"),
        P("gx", "gy", "gz"),
        *([P()] * 8),
    )
    return jax.shard_map(
        shards,
        mesh=mesh,
        in_specs=placed,
        out_specs=P("gx", "gy", "gz", None, None),
        check_vma=False,
    )
```

time: 54.7 us -> 38.7 us (0.71)
  Pallas kernels: 20 us -> 11.7 us
  local copies, waits for them, and re-layouts: 6.17 us -> 0.91 us
  starting transfers between devices: 18.3 us -> 16.6 us
    pallas_call x4 -> x7, Pallas kernels: 20 us -> 11.7 us  [the longest x2 8.74 us: run_late(): return call(body, outs, specs)(*args)]
    unnamed x28 -> x22, local copies, waits for them, and re-layouts: 6.17 us -> 0.91 us
    ppermute x9, starting transfers between devices: 18 us -> 16.2 us  [the longest x4 8.53 us: exchange(): lax.ppermute(block, 'gy', swaps(lax.axis_size('gy'), parity, around))]
    ppermute x9, waiting for transfers between devices: 5.93 us -> 5.09 us  [the longest x4 3.41 us: exchange(): lax.ppermute(block, 'gy', swaps(lax.axis_size('gy'), parity, around))]
  transfers between devices with their start and end apart: 10 -> 10, of which waited for: 3 -> 4; matrix products, arithmetic and copies ran while one was open for 0% -> 0% of each run, Pallas kernels for 0% -> 6%
where the time goes in v2:
time: 38.7 us; the launch traced here: 38.5 us
  starting transfers between devices  16.6 us (43%)
  Pallas kernels  11.7 us (30%)
  waiting for transfers between devices  9.17 us (24%)
  local copies, waits for them, and re-layouts  0.91 us (2%)
    pallas_call x2, Pallas kernels, run_late(): return call(body, outs, specs)(*args)  8.74 us
    ppermute x4, starting transfers between devices, exchange(): lax.ppermute(block, 'gy', swaps(lax.axis_size('gy'), parity, around))  8.53 us
    ppermute x5, starting transfers between devices, exchange(): block = lax.ppermute(own, axis, pairs)  7.64 us
    ppermute x1, waiting for transfers between devices, shards(): arrived = lax.ppermute(travel, 'gz', swaps(depth, 0))  4.08 us
    ppermute x4, waiting for transfers between devices, exchange(): lax.ppermute(block, 'gy', swaps(lax.axis_size('gy'), parity, around))  3.41 us
    pallas_call x2, Pallas kernels, run_early(): return call(body, outs, [VMEM] * (4 + len(near)))(own, *near, *weights[:3])  2.29 us
    ppermute x5, waiting for transfers between devices, exchange(): block = lax.ppermute(own, axis, pairs)  1.68 us
    unnamed x22, local copies, waits for them, and re-layouts  0.91 us
  transfers between devices with their start and end apart: 10, of which 4 were waited for; matrix products, arithmetic and copies ran while one was open for 0% of the time, Pallas kernels for 6%

profile of v2, /device:TPU:1, one launch (start us, length us, event | category | flops | bytes accessed | tf_op | source)
XLA Modules:
  0.0 38.5 jit_solution(11706686440024461247)
XLA Ops:
  0.0 0.0 copy-start.9
  0.0 0.0 copy-start.6
  0.0 0.0 copy-start.2
  0.0 0.0 copy-start.1
  0.0 0.0 copy-start
  0.0 0.0 copy-start.4
  0.0 0.0 copy-start.3
  0.0 0.0 copy-start.5
  0.1 0.0 copy-start.8
  0.1 0.0 copy-start.7
  0.1 0.0 copy-start.10
  0.1 0.6 %copy-done.9 = s32[1,2,1]{1,2,0:T(1,128)S(1)} copy-done((s32[1,2,1]{1,2,0:T(1,128)S(1)}, s32[1,2,1]{1,2,0:T(1,128)}, u32[]{:S(2)}) %copy-start.9) | copy-done | bytes 32
  0.7 0.3 copy-done.6
  1.0 0.6 %shard_map.109 = (bf16[2,144,256]{2,1,0:T(8,128)(2,1)S(1)}, bf16[144,256]{1,0:T(8,128)(2,1)S(1)}, bf16[144,256]{1,0:T(8,128)(2,1)S(1)}, f32[2,128,256]{2,1,0:T(8,128)S(1)}) custom-call(f32[2,128,256]{2,1,0:T(8,128)S(1)} %bitcast.8, s32[2]{0:T(128)S(1)} %bitcast.13, f32[8,128]{1,0:T(8,128)S(1)} %prepare.1.ready), custom_call_target="tpu_custom_call" | custom-call | tf_op jit(solution)/shard_map/pallas_call | solution.py:110
  1.6 2.1 %collective-permute-start.2 = (bf16[2,144,256]{2,1,0:T(8,128)(2,1)S(1)}, bf16[2,144,256]{2,1,0:T(8,128)(2,1)S(1)}, u32[]{:S(2)}, u32[]{:S(2)}) collective-permute-start(bf16[2,144,256]{2,1,0:T(8,128)(2,1)S(1)} %get-tuple-element.27.own.refs_1_), channel_id=1, source_target_pairs={{0,1},{1,0},{2,3},{3,2},{4,5},{5,4},{6,7},{7,6},{8,9},{9,8},{10,11... | collective-permute-start | bytes 442376 | tf_op jit(solution)/shard_map/ppermute | solution.py:375
  3.7 3.3 %collective-permute-start.1 = (bf16[2,144,256]{2,1,0:T(8,128)(2,1)S(1)}, bf16[2,144,256]{2,1,0:T(8,128)(2,1)S(1)}, u32[]{:S(2)}, u32[]{:S(2)}) collective-permute-start(bf16[2,144,256]{2,1,0:T(8,128)(2,1)S(1)} %get-tuple-element.27.own.refs_1_), channel_id=1, source_target_pairs={{8,16},{16,8},{0,24},{24,0},{9,17},{17,9},{1,25},{25,1},{10,18},{1... | collective-permute-start | bytes 442376 | tf_op jit(solution)/shard_map/ppermute | solution.py:375
  7.0 0.0 collective-permute-start
  7.0 1.2 %collective-permute-start.3 = (bf16[144,256]{1,0:T(8,128)(2,1)S(1)}, bf16[144,256]{1,0:T(8,128)(2,1)S(1)}, u32[]{:S(2)}, u32[]{:S(2)}) collective-permute-start(bf16[144,256]{1,0:T(8,128)(2,1)S(1)} %get-tuple-element.28), channel_id=1, source_target_pairs={{0,2},{2,0},{4,6},{6,4},{1,3},{3,1},{5,7},{7,5},{8,10},{10,8},{12,... | collective-permute-start | bytes 221192 | tf_op jit(solution)/shard_map/ppermute | solution.py:380
  8.2 1.1 %collective-permute-start.4 = (bf16[144,256]{1,0:T(8,128)(2,1)S(1)}, bf16[144,256]{1,0:T(8,128)(2,1)S(1)}, u32[]{:S(2)}, u32[]{:S(2)}) collective-permute-start(bf16[144,256]{1,0:T(8,128)(2,1)S(1)} %get-tuple-element.29), channel_id=1, source_target_pairs={{2,4},{4,2},{0,6},{6,0},{3,5},{5,3},{1,7},{7,1},{10,12},{12,10},{8... | collective-permute-start | bytes 221192 | tf_op jit(solution)/shard_map/ppermute | solution.py:380
  9.3 0.0 copy-done.2
  9.4 0.0 copy-done.1
  9.4 0.0 copy-done
  9.4 1.0 %shard_map.110 = (bf16[2,256,256]{2,1,0:T(8,128)(2,1)S(1)}, bf16[8,256,256]{2,1,0:T(8,128)(2,1)S(1)}, f32[8,256,256]{2,1,0:T(8,128)S(1)}, f32[8,1,256]{2,1,0:T(1,128)S(1)}, f32[8,1,256]{2,1,0:T(1,128)S(1)}) custom-call(bf16[2,144,256]{2,1,0:T(8,128)(2,1)S(1)} %get-tuple-element.27.own.refs_1_, bf16[256,256]{1,0:T(8,128)(2,1)S(1)} %copy-done, ...), custom_call_target="tpu_custom_call" | custom-call | tf_op jit(solution)/shard_map/pallas_call | solution.py:189
  10.3 0.0 collective-permute-done.3.refs_5_
  10.3 2.1 %collective-permute-done.4.refs_6_ = bf16[144,256]{1,0:T(8,128)(2,1)S(1)} collective-permute-done((bf16[144,256]{1,0:T(8,128)(2,1)S(1)}, bf16[144,256]{1,0:T(8,128)(2,1)S(1)}, u32[]{:S(2)}, u32[]{:S(2)}) %collective-permute-start.4) | collective-permute-done | bytes 73760 | tf_op jit(solution)/shard_map/ppermute | solution.py:380
  12.4 0.0 collective-permute-done.2.refs_4_
  12.4 0.0 collective-permute-done.1.refs_3_
  12.4 1.7 %collective-permute-done.refs_2_ = bf16[2,144,256]{2,1,0:T(8,128)(2,1)S(1)} collective-permute-done((bf16[2,144,256]{2,1,0:T(8,128)(2,1)S(1)}, bf16[2,144,256]{2,1,0:T(8,128)(2,1)S(1)}, u32[]{:S(2)}, u32[]{:S(2)}) %collective-permute-start) | collective-permute-done | bytes 147488 | tf_op jit(solution)/shard_map/ppermute | solution.py:375
  14.1 0.0 copy-done.4
  14.1 0.0 copy-done.3
  14.1 0.0 copy-done.5
  14.1 0.0 copy-done.8
  14.1 0.0 copy-done.7
  14.1 0.0 copy-done.10
  14.1 5.0 %shard_map.111 = (bf16[2,144,256]{2,1,0:T(8,128)(2,1)S(1)}, f32[128,256]{1,0:T(8,128)S(1)}) custom-call(f32[2,128,256]{2,1,0:T(8,128)S(1)} %get-tuple-element.26.refs_0_, bf16[2,144,256]{2,1,0:T(8,128)(2,1)S(1)} %get-tuple-element.27.own.refs_1_, bf16[2,144,256]{2,1,0:T(8,128)(2,1)S(1)} %collective-permute-done.refs_2_, ...), custom_call_target="tpu_custom_call" | custom-call | tf_op jit(solution)/shard_map/pallas_call | solution.py:308
  19.1 0.4 %collective-permute-start.5 = (bf16[2,144,256]{2,1,0:T(8,128)(2,1)S(1)}, bf16[2,144,256]{2,1,0:T(8,128)(2,1)S(1)}, u32[]{:S(2)}, u32[]{:S(2)}) collective-permute-start(bf16[2,144,256]{2,1,0:T(8,128)(2,1)S(1)} %get-tuple-element.35.travel), channel_id=1, source_target_pairs={{0,1},{1,0},{2,3},{3,2},{4,5},{5,4},{6,7},{7,6},{8,9},{9,8},{10,11... | collective-permute-start | bytes 442376 | tf_op jit(solution)/shard_map/ppermute | solution.py:405
  19.5 4.1 %collective-permute-done.5.arrived = bf16[2,144,256]{2,1,0:T(8,128)(2,1)S(1)} collective-permute-done((bf16[2,144,256]{2,1,0:T(8,128)(2,1)S(1)}, bf16[2,144,256]{2,1,0:T(8,128)(2,1)S(1)}, u32[]{:S(2)}, u32[]{:S(2)}) %collective-permute-start.5) | collective-permute-done | bytes 147488 | tf_op jit(solution)/shard_map/ppermute | solution.py:405
  23.6 0.1 shard_map.112
  23.7 0.7 %collective-permute-start.7 = (bf16[2,144,256]{2,1,0:T(8,128)(2,1)S(1)}, bf16[2,144,256]{2,1,0:T(8,128)(2,1)S(1)}, u32[]{:S(2)}, u32[]{:S(2)}) collective-permute-start(bf16[2,144,256]{2,1,0:T(8,128)(2,1)S(1)} %get-tuple-element.38.own.refs_1_), channel_id=1, source_target_pairs={{8,16},{16,8},{9,17},{17,9},{10,18},{18,10},{11,19},{19,11},{12,20... | collective-permute-start | bytes 442376 | tf_op jit(solution)/shard_map/ppermute | solution.py:375
  24.4 1.5 %collective-permute-start.6 = (bf16[2,144,256]{2,1,0:T(8,128)(2,1)S(1)}, bf16[2,144,256]{2,1,0:T(8,128)(2,1)S(1)}, u32[]{:S(2)}, u32[]{:S(2)}) collective-permute-start(bf16[2,144,256]{2,1,0:T(8,128)(2,1)S(1)} %get-tuple-element.38.own.refs_1_), channel_id=1, source_target_pairs={{0,8},{8,0},{16,24},{24,16},{1,9},{9,1},{17,25},{25,17},{2,10},{10... | collective-permute-start | bytes 442376 | tf_op jit(solution)/shard_map/ppermute | solution.py:375
  25.9 3.2 %collective-permute-start.8 = (bf16[144,256]{1,0:T(8,128)(2,1)S(1)}, bf16[144,256]{1,0:T(8,128)(2,1)S(1)}, u32[]{:S(2)}, u32[]{:S(2)}) collective-permute-start(bf16[144,256]{1,0:T(8,128)(2,1)S(1)} %get-tuple-element.39), channel_id=1, source_target_pairs={{0,2},{2,0},{4,6},{6,4},{1,3},{3,1},{5,7},{7,5},{8,10},{10,8},{12,... | collective-permute-start | bytes 221192 | tf_op jit(solution)/shard_map/ppermute | solution.py:380
  29.1 3.0 %collective-permute-start.9 = (bf16[144,256]{1,0:T(8,128)(2,1)S(1)}, bf16[144,256]{1,0:T(8,128)(2,1)S(1)}, u32[]{:S(2)}, u32[]{:S(2)}) collective-permute-start(bf16[144,256]{1,0:T(8,128)(2,1)S(1)} %get-tuple-element.40), channel_id=1, source_target_pairs={{2,4},{4,2},{3,5},{5,3},{10,12},{12,10},{11,13},{13,11},{18,20},{2... | collective-permute-start | bytes 221192 | tf_op jit(solution)/shard_map/ppermute | solution.py:380
  32.1 1.3 %shard_map.113 = (bf16[2,256,384]{2,1,0:T(8,128)(2,1)S(1)}, bf16[8,256,256]{2,1,0:T(8,128)(2,1)S(1)}, f32[8,384,256]{2,1,0:T(8,128)S(1)}, f32[8,1,256]{2,1,0:T(1,128)S(1)}, f32[8,1,256]{2,1,0:T(1,128)S(1)}) custom-call(bf16[2,144,256]{2,1,0:T(8,128)(2,1)S(1)} %get-tuple-element.38.own.refs_1_, bf16[2,144,256]{2,1,0:T(8,128)(2,1)S(1)} %get-tuple-element.41.refs_0_, ...), custom_call_target="tpu_custom_call" | custom-call | tf_op jit(solution)/shard_map/pallas_call | solution.py:189
  33.4 0.0 collective-permute-done.8.refs_4_
  33.4 1.3 %collective-permute-done.9.refs_5_ = bf16[144,256]{1,0:T(8,128)(2,1)S(1)} collective-permute-done((bf16[144,256]{1,0:T(8,128)(2,1)S(1)}, bf16[144,256]{1,0:T(8,128)(2,1)S(1)}, u32[]{:S(2)}, u32[]{:S(2)}) %collective-permute-start.9) | collective-permute-done | bytes 73760 | tf_op jit(solution)/shard_map/ppermute | solution.py:380
  34.7 0.0 collective-permute-done.7.refs_3_
  34.7 0.0 collective-permute-done.6.refs_2_
  34.8 3.8 %shard_map.114 = f32[2,128,256]{2,1,0:T(8,128)} custom-call(f32[2,128,256]{2,1,0:T(8,128)S(1)} %get-tuple-element.37.refs_0_, bf16[2,144,256]{2,1,0:T(8,128)(2,1)S(1)} %get-tuple-element.38.own.refs_1_, bf16[2,144,256]{2,1,0:T(8,128)(2,1)S(1)} %collective-permute-done.6.refs_2_, bf16[2,144,256]{2,1,0:T(8,128)(2,1)S(1)} %collective-permute-done.7.refs_3_, ...), custom_call_target="tpu_custom_call" | custom-call | tf_op jit(solution)/shard_map/pallas_call | solution.py:308
  (1 shorter events, 0.0 us)
Async XLA Ops:
  0.0 0.7 %copy-start.9 = (s32[1,2,1]{1,2,0:T(1,128)S(1)}, s32[1,2,1]{1,2,0:T(1,128)}, u32[]{:S(2)}) copy-start(s32[1,2,1]{1,2,0:T(1,128)} %param.12) | copy-start | bytes 28
  0.0 1.0 %copy-start.6 = (f32[1,2,1,128,256]{4,3,2,1,0:T(8,128)S(1)}, f32[1,2,1,128,256]{4,3,2,1,0:T(8,128)}, u32[]{:S(2)}) copy-start(f32[1,2,1,128,256]{4,3,2,1,0:T(8,128)} %param.11) | copy-start | bytes 786436
  0.0 9.3 %copy-start.2 = (bf16[256,256]{1,0:T(8,128)(2,1)S(1)}, bf16[256,256]{1,0:T(8,128)(2,1)}, u32[]{:S(2)}) copy-start(bf16[256,256]{1,0:T(8,128)(2,1)} %refs_13_.3) | copy-start | bytes 393220
  0.0 9.3 %copy-start.1 = (bf16[256,256]{1,0:T(8,128)(2,1)S(1)}, bf16[256,256]{1,0:T(8,128)(2,1)}, u32[]{:S(2)}) copy-start(bf16[256,256]{1,0:T(8,128)(2,1)} %refs_12_.3) | copy-start | bytes 393220
  0.0 9.3 %copy-start = (bf16[256,256]{1,0:T(8,128)(2,1)S(1)}, bf16[256,256]{1,0:T(8,128)(2,1)}, u32[]{:S(2)}) copy-start(bf16[256,256]{1,0:T(8,128)(2,1)} %refs_11_.1) | copy-start | bytes 393220
  0.0 14.1 %copy-start.4 = (bf16[1024,256]{1,0:T(8,128)(2,1)S(1)}, bf16[1024,256]{1,0:T(8,128)(2,1)}, u32[]{:S(2)}) copy-start(bf16[1024,256]{1,0:T(8,128)(2,1)} %refs_16_.3) | copy-start | bytes 1572868
  0.0 14.1 %copy-start.3 = (bf16[256,1024]{1,0:T(8,128)(2,1)S(1)}, bf16[256,1024]{1,0:T(8,128)(2,1)}, u32[]{:S(2)}) copy-start(bf16[256,1024]{1,0:T(8,128)(2,1)} %refs_15_.3) | copy-start | bytes 1572868
  0.0 14.1 %copy-start.5 = (bf16[256,256]{1,0:T(8,128)(2,1)S(1)}, bf16[256,256]{1,0:T(8,128)(2,1)}, u32[]{:S(2)}) copy-start(bf16[256,256]{1,0:T(8,128)(2,1)} %refs_14_.3) | copy-start | bytes 393220
  0.1 14.1 %copy-start.8 = (f32[256]{0:T(256)S(1)}, f32[256]{0:T(256)}, u32[]{:S(2)}) copy-start(f32[256]{0:T(256)} %param.21) | copy-start | bytes 3076
  0.1 14.1 %copy-start.7 = (f32[256]{0:T(256)S(1)}, f32[256]{0:T(256)}, u32[]{:S(2)}) copy-start(f32[256]{0:T(256)} %param.20) | copy-start | bytes 3076
  0.1 14.1 %copy-start.10 = (s32[1,2,1]{1,2,0:T(1,128)S(1)}, s32[1,2,1]{1,2,0:T(1,128)}, u32[]{:S(2)}) copy-start(s32[1,2,1]{1,2,0:T(1,128)} %param.13) | copy-start | bytes 28
  1.6 10.9 %collective-permute-start.2 = (bf16[2,144,256]{2,1,0:T(8,128)(2,1)S(1)}, bf16[2,144,256]{2,1,0:T(8,128)(2,1)S(1)}, u32[]{:S(2)}, u32[]{:S(2)}) collective-permute-start(bf16[2,144,256]{2,1,0:T(8,128)(2,1)S(1)} %get-tuple-element.27.own.refs_1_), channel_id=1, source_target_pairs={{0,1},{1,0},{2,3},{3,2},{4,5},{5,4},{6,7},{7,6},{8,9},{9,8},{10,11... | collective-permute-start | bytes 442376 | tf_op jit(solution)/shard_map/ppermute | solution.py:375
  3.7 8.7 %collective-permute-start.1 = (bf16[2,144,256]{2,1,0:T(8,128)(2,1)S(1)}, bf16[2,144,256]{2,1,0:T(8,128)(2,1)S(1)}, u32[]{:S(2)}, u32[]{:S(2)}) collective-permute-start(bf16[2,144,256]{2,1,0:T(8,128)(2,1)S(1)} %get-tuple-element.27.own.refs_1_), channel_id=1, source_target_pairs={{8,16},{16,8},{0,24},{24,0},{9,17},{17,9},{1,25},{25,1},{10,18},{1... | collective-permute-start | bytes 442376 | tf_op jit(solution)/shard_map/ppermute | solution.py:375
  7.0 7.1 %collective-permute-start = (bf16[2,144,256]{2,1,0:T(8,128)(2,1)S(1)}, bf16[2,144,256]{2,1,0:T(8,128)(2,1)S(1)}, u32[]{:S(2)}, u32[]{:S(2)}) collective-permute-start(bf16[2,144,256]{2,1,0:T(8,128)(2,1)S(1)} %get-tuple-element.27.own.refs_1_), channel_id=1, source_target_pairs={{0,8},{8,0},{16,24},{24,16},{1,9},{9,1},{17,25},{25,17},{2,10},{10... | collective-permute-start | bytes 442376 | tf_op jit(solution)/shard_map/ppermute | solution.py:375
  7.0 3.3 %collective-permute-start.3 = (bf16[144,256]{1,0:T(8,128)(2,1)S(1)}, bf16[144,256]{1,0:T(8,128)(2,1)S(1)}, u32[]{:S(2)}, u32[]{:S(2)}) collective-permute-start(bf16[144,256]{1,0:T(8,128)(2,1)S(1)} %get-tuple-element.28), channel_id=1, source_target_pairs={{0,2},{2,0},{4,6},{6,4},{1,3},{3,1},{5,7},{7,5},{8,10},{10,8},{12,... | collective-permute-start | bytes 221192 | tf_op jit(solution)/shard_map/ppermute | solution.py:380
  8.2 4.2 %collective-permute-start.4 = (bf16[144,256]{1,0:T(8,128)(2,1)S(1)}, bf16[144,256]{1,0:T(8,128)(2,1)S(1)}, u32[]{:S(2)}, u32[]{:S(2)}) collective-permute-start(bf16[144,256]{1,0:T(8,128)(2,1)S(1)} %get-tuple-element.29), channel_id=1, source_target_pairs={{2,4},{4,2},{0,6},{6,0},{3,5},{5,3},{1,7},{7,1},{10,12},{12,10},{8... | collective-permute-start | bytes 221192 | tf_op jit(solution)/shard_map/ppermute | solution.py:380
  19.1 4.5 %collective-permute-start.5 = (bf16[2,144,256]{2,1,0:T(8,128)(2,1)S(1)}, bf16[2,144,256]{2,1,0:T(8,128)(2,1)S(1)}, u32[]{:S(2)}, u32[]{:S(2)}) collective-permute-start(bf16[2,144,256]{2,1,0:T(8,128)(2,1)S(1)} %get-tuple-element.35.travel), channel_id=1, source_target_pairs={{0,1},{1,0},{2,3},{3,2},{4,5},{5,4},{6,7},{7,6},{8,9},{9,8},{10,11... | collective-permute-start | bytes 442376 | tf_op jit(solution)/shard_map/ppermute | solution.py:405
  23.7 11.0 %collective-permute-start.7 = (bf16[2,144,256]{2,1,0:T(8,128)(2,1)S(1)}, bf16[2,144,256]{2,1,0:T(8,128)(2,1)S(1)}, u32[]{:S(2)}, u32[]{:S(2)}) collective-permute-start(bf16[2,144,256]{2,1,0:T(8,128)(2,1)S(1)} %get-tuple-element.38.own.refs_1_), channel_id=1, source_target_pairs={{8,16},{16,8},{9,17},{17,9},{10,18},{18,10},{11,19},{19,11},{12,20... | collective-permute-start | bytes 442376 | tf_op jit(solution)/shard_map/ppermute | solution.py:375
  24.4 10.4 %collective-permute-start.6 = (bf16[2,144,256]{2,1,0:T(8,128)(2,1)S(1)}, bf16[2,144,256]{2,1,0:T(8,128)(2,1)S(1)}, u32[]{:S(2)}, u32[]{:S(2)}) collective-permute-start(bf16[2,144,256]{2,1,0:T(8,128)(2,1)S(1)} %get-tuple-element.38.own.refs_1_), channel_id=1, source_target_pairs={{0,8},{8,0},{16,24},{24,16},{1,9},{9,1},{17,25},{25,17},{2,10},{10... | collective-permute-start | bytes 442376 | tf_op jit(solution)/shard_map/ppermute | solution.py:375
  25.9 7.5 %collective-permute-start.8 = (bf16[144,256]{1,0:T(8,128)(2,1)S(1)}, bf16[144,256]{1,0:T(8,128)(2,1)S(1)}, u32[]{:S(2)}, u32[]{:S(2)}) collective-permute-start(bf16[144,256]{1,0:T(8,128)(2,1)S(1)} %get-tuple-element.39), channel_id=1, source_target_pairs={{0,2},{2,0},{4,6},{6,4},{1,3},{3,1},{5,7},{7,5},{8,10},{10,8},{12,... | collective-permute-start | bytes 221192 | tf_op jit(solution)/shard_map/ppermute | solution.py:380
  29.1 5.7 %collective-permute-start.9 = (bf16[144,256]{1,0:T(8,128)(2,1)S(1)}, bf16[144,256]{1,0:T(8,128)(2,1)S(1)}, u32[]{:S(2)}, u32[]{:S(2)}) collective-permute-start(bf16[144,256]{1,0:T(8,128)(2,1)S(1)} %get-tuple-element.40), channel_id=1, source_target_pairs={{2,4},{4,2},{3,5},{5,3},{10,12},{12,10},{11,13},{13,11},{18,20},{2... | collective-permute-start | bytes 221192 | tf_op jit(solution)/shard_map/ppermute | solution.py:380
